TPU v7x, 128 devices: a whole 4x4x4 slice. The times are simulated.
128 devices in a mesh: slab: 8 (over x, y_lo), tile: 16 (over y_hi, z, core).
Axes of the slice: x: 4, y: 4 (y_hi: 2, y_lo: 2; y = y_hi * 2 + y_lo), z: 4, core: 2. Of those that a mesh axis runs over, the one named last changes fastest.
Arguments:
- distribution_functions: float32 [19, 128, 512, 128], P(None, 'slab', 'tile')
- heat_excess_scalar: float32 [128, 512, 128], P('slab', 'tile'), may hold values from -6 to 6
- obstacle_site_flag: int32 [128, 512, 128], P('slab', 'tile'), may hold values from 0 to 1, as said below
- cabinet_category_label: int32 [1024], replicated, may hold values from 0 to 7
- intake_face_position: int32 [1024, 32], replicated, may hold values from 0 to 8388607, as said below
- outflow_face_position: int32 [1024, 32], replicated, may hold values from 0 to 8388607, as said below
- category_evolution_operator: bfloat16 [8, 2048, 2048], P(None, 'tile', 'slab'), may hold values from -0.125 to 0.125
- intake_input_coefficients: float32 [8, 2048], replicated, may hold values from -12 to 12
- outflow_output_coefficients: float32 [8, 2048], replicated, may hold values from -0.125 to 0.125
- cabinet_heat_vector: bfloat16 [1024, 2048], P('slab'), may hold values from -6 to 6
Outputs:
- new_populations: float32 [19, 128, 512, 128], P(None, 'slab', 'tile')
- new_temperature: float32 [128, 512, 128], P('slab', 'tile')
- new_states: float32 [1024, 2048], P('slab', 'tile')
Inputs may be any that keep to these rules, and one draw needn't show every extreme that they name: `intake_face_position`: each rack is a block 4 cells wide and 8 high in a row of racks along the hall; its inlet face, body and exhaust face lie in three consecutive cells along the hall's length, all within one slab of 16 cells. No cell belongs to two faces; face cells are never solid. `outflow_face_position`: same layout as the inlet faces, two cells further along the hall. `obstacle_site_flag`: the lowest and highest layer of cells and every rack body are solid.
All inputs are finite; a program needn't handle non-finite values.
Results may differ from a plain program's by a relative error of at most 0.00085.
Values may be sent and summed in bfloat16 or wider, within the bound.
A program may use at most 128 MiB of HBM per device.

v0:
```python
import jax
import jax.numpy as jnp
from jax import lax
from jax.sharding import PartitionSpec as P

STEPS = 3


VELOCITY = (
    (0, 0, 0),
    (1, 0, 0),
    (-1, 0, 0),
    (0, 1, 0),
    (0, -1, 0),
    (0, 0, 1),
    (0, 0, -1),
    (1, 1, 0),
    (-1, -1, 0),
    (1, -1, 0),
    (-1, 1, 0),
    (1, 0, 1),
    (-1, 0, -1),
    (1, 0, -1),
    (-1, 0, 1),
    (0, 1, 1),
    (0, -1, -1),
    (0, 1, -1),
    (0, -1, 1),
)
OPPOSITE = (0, 2, 1, 4, 3, 6, 5, 8, 7, 10, 9, 12, 11, 14, 13, 16, 15, 18, 17)
WEIGHTS = (1.0 / 3.0,) + (1.0 / 18.0,) * 6 + (1.0 / 36.0,) * 12
relax_time = 0.6
buoyancy = 0.01
diffusion = 0.1
mixing = 0.5
keep_share = 0.5


def extended(cells, sides, width):
    for axis, dim in sides:
        count = lax.axis_size(axis)
        head = lax.slice_in_dim(cells, 0, width, axis=dim)
        tail = lax.slice_in_dim(cells, cells.shape[dim] - width, cells.shape[dim], axis=dim)
        cells = jnp.concatenate(
            [
                lax.ppermute(tail, axis, [(i, (i + 1) % count) for i in range(count)]),
                cells,
                lax.ppermute(head, axis, [((i + 1) % count, i) for i in range(count)]),
            ],
            axis=dim,
        )
    return cells


def collide(lattice_quantities, heated_quantities, solid):
    density = jnp.sum(lattice_quantities, axis=0)
    velocity = []
    for dimension in range(3):
        summed = jnp.zeros_like(density)
        for lane in range(19):
            stride = VELOCITY[lane][dimension]
            if stride != 0:
                summed = summed + stride * lattice_quantities[lane]
        velocity.append(summed / density)
    shifted = [
        velocity[0],
        velocity[1],
        velocity[2] + relax_time * buoyancy * heated_quantities / density,
    ]
    speed_sq = shifted[0] * shifted[0] + shifted[1] * shifted[1] + shifted[2] * shifted[2]
    relaxed = []
    for lane in range(19):
        stride = VELOCITY[lane]
        projected = stride[0] * shifted[0] + stride[1] * shifted[1] + stride[2] * shifted[2]
        balance = (
            WEIGHTS[lane]
            * density
            * (1.0 + 3.0 * projected + 4.5 * projected * projected - 1.5 * speed_sq)
        )
        relaxed_lane = lattice_quantities[lane] - (lattice_quantities[lane] - balance) / relax_time
        relaxed.append(jnp.where(solid, lattice_quantities[OPPOSITE[lane]], relaxed_lane))
    return (jnp.stack(relaxed), velocity)


def heat_step(centre, neighbours, velocity, solid):
    laplace = -6.0 * centre
    carried = jnp.zeros_like(centre)
    for dimension in range(3):
        behind, ahead = neighbours[dimension]
        laplace = laplace + behind + ahead
        carried = carried + velocity[dimension] * (0.5 * (ahead - behind))
    return jnp.where(solid, centre, centre + diffusion * laplace - carried)


def advance(relaxed_pad, heat_pad, velocity, solid):
    size_x = solid.shape[0]
    size_y = solid.shape[1]
    passed = []
    for lane in range(19):
        stride = VELOCITY[lane]
        moved = relaxed_pad[
            lane, 1 - stride[0] : 1 - stride[0] + size_x, 1 - stride[1] : 1 - stride[1] + size_y
        ]
        passed.append(jnp.roll(moved, stride[2], axis=2))
    centre = heat_pad[1 : 1 + size_x, 1 : 1 + size_y]
    neighbours = (
        (heat_pad[0:size_x, 1 : 1 + size_y], heat_pad[2 : 2 + size_x, 1 : 1 + size_y]),
        (heat_pad[1 : 1 + size_x, 0:size_y], heat_pad[1 : 1 + size_x, 2 : 2 + size_y]),
        (jnp.roll(centre, 1, axis=2), jnp.roll(centre, -1, axis=2)),
    )
    return (jnp.stack(passed), heat_step(centre, neighbours, velocity, solid))


def select(products, kind_hot, rows_here):
    shaped = products.reshape(products.shape[0], kind_hot.shape[1], rows_here)
    return jnp.sum(shaped * kind_hot[:, :, None], axis=1)


def per_device(
    distribution_functions,
    heat_excess_scalar,
    obstacle_site_flag,
    cabinet_category_label,
    intake_face_position,
    outflow_face_position,
    category_evolution_operator,
    intake_input_coefficients,
    outflow_output_coefficients,
    cabinet_heat_vector,
):
    solid = obstacle_site_flag == 1
    lattice_quantities, heated_quantities = (distribution_functions, heat_excess_scalar)
    for substep in range(STEPS):
        relaxed, velocity = collide(lattice_quantities, heated_quantities, solid)
        stacked = jnp.concatenate((relaxed, heated_quantities[None]), axis=0)
        padded = extended(stacked, (("slab", 1), ("tile", 2)), 1)
        lattice_quantities, heated_quantities = advance(padded[:19], padded[19], velocity, solid)
    slab_index = lax.axis_index("slab")
    tile_index = lax.axis_index("tile")
    size_x, size_y, height = heated_quantities.shape
    across_total = size_y * lax.axis_size("tile")
    block_racks = cabinet_heat_vector.shape[0]
    kinds_count = category_evolution_operator.shape[0]
    rows_here = category_evolution_operator.shape[1]
    first_rack = slab_index * block_racks
    kind_range = jnp.arange(kinds_count, dtype=jnp.int32)
    block_types = lax.dynamic_slice_in_dim(cabinet_category_label, first_rack, block_racks)
    kind_hot = (block_types[:, None] == kind_range[None, :]).astype(jnp.float32)

    def locate(face_cells):
        pos_x = face_cells // (across_total * height)
        remain = face_cells % (across_total * height)
        pos_y = remain // height
        pos_z = remain % height
        owned = (pos_x // size_x == slab_index) & (pos_y // size_y == tile_index)
        local_index = (
            (pos_x - slab_index * size_x) * size_y + (pos_y - tile_index * size_y)
        ) * height + pos_z
        return (owned, jnp.where(owned, local_index, 0))

    flat_heat = heated_quantities.reshape(-1)
    block_inlet = lax.dynamic_slice_in_dim(intake_face_position, first_rack, block_racks, 0)
    inlet_owned, inlet_index = locate(block_inlet)
    partial_inlet = jnp.sum(jnp.where(inlet_owned, flat_heat[inlet_index], 0.0), axis=1)
    inlet_mean = lax.psum(partial_inlet, "tile") / intake_face_position.shape[1]
    piece_cols = lax.all_gather(category_evolution_operator, "slab", axis=2, tiled=True)
    flat_piece = piece_cols.reshape(kinds_count * rows_here, piece_cols.shape[2])
    all_kinds = lax.dot_general(
        cabinet_heat_vector,
        flat_piece,
        (((1,), (1,)), ((), ())),
        preferred_element_type=jnp.float32,
    )
    mixed = select(all_kinds, kind_hot, rows_here)
    first_row = tile_index * rows_here
    state_rows = lax.dynamic_slice_in_dim(cabinet_heat_vector, first_row, rows_here, 1).astype(
        jnp.float32
    )
    gain_table = lax.dynamic_slice_in_dim(intake_input_coefficients, first_row, rows_here, 1)
    read_table = lax.dynamic_slice_in_dim(outflow_output_coefficients, first_row, rows_here, 1)
    gain_rows = jnp.dot(kind_hot, gain_table, precision=lax.Precision.HIGHEST)
    read_rows = jnp.dot(kind_hot, read_table, precision=lax.Precision.HIGHEST)
    new_states = keep_share * state_rows + mixed + gain_rows * inlet_mean[:, None]
    partial_exhaust = jnp.sum(read_rows * new_states, axis=1)
    exhaust = lax.psum(partial_exhaust, "tile")
    block_exhaust = lax.dynamic_slice_in_dim(outflow_face_position, first_rack, block_racks, 0)
    exhaust_owned, exhaust_index = locate(block_exhaust)
    old_values = flat_heat[exhaust_index]
    change = jnp.where(exhaust_owned, mixing * (exhaust[:, None] - old_values), 0.0)
    flat_heat = flat_heat.at[exhaust_index.reshape(-1)].add(change.reshape(-1))
    return (lattice_quantities, flat_heat.reshape(heated_quantities.shape), new_states)


def solution(mesh):
    return jax.shard_map(
        per_device,
        mesh=mesh,
        in_specs=(
            P(None, "slab", "tile", None),
            P("slab", "tile", None),
            P("slab", "tile", None),
            P(),
            P(),
            P(),
            P(None, "tile", "slab"),
            P(),
            P(),
            P("slab", None),
        ),
        out_specs=(P(None, "slab", "tile", None), P("slab", "tile", None), P("slab", "tile")),
        check_vma=False,
    )
```

profile of v0, /device:TPU:1, one launch (start us, length us, event | category | flops | bytes accessed | tf_op | source)
XLA Modules:
  0.0 353.2 jit_solution(3612530613693756231)
XLA Ops:
  7.2 3.0 reduce_sum.184
  10.3 4.1 %bitcast_dynamic-update-slice_fusion.10 = (f32[20,16,32,128]{3,2,1,0:T(8,128)S(1)}, f32[16,32,128]{2,1,0:T(8,128)}, f32[16,32,128]{2,1,0:T(8,128)S(1)}, f32[16,3...) fusion(f32[16,32,128]{2,1,0:T(8,128)S(1)} %reduce_sum.184, ...), kind=kLoop, calls=%fused_computation.703 | loop fusion | flops 4521983 | bytes 7667712
  19.7 2.3 copy-done.4
  24.3 2.3 collective-permute-start.1
  29.0 9.2 %collective-permute-done = f32[20,1,32,128]{3,2,1,0:T(8,128)S(1)} collective-permute-done((f32[20,1,32,128]{3,2,1,0:T(8,128)S(1)}, f32[20,1,32,128]{3,2,1,0:T(8,128)S(1)}, u32[]{:S(2)}, u32[]{:S(2)}) %collective-permute-start) | collective-permute-done | bytes 327712 | tf_op jit(solution)/shard_map/ppermute | solution.py:46
  38.2 2.8 collective-permute-done.1
  41.0 2.9 pad_maximum_fusion.70
  43.9 10.6 %collective-permute-start.2 = (f32[20,18,1,128]{3,2,1,0:T(1,128)}, f32[20,18,1,128]{3,2,1,0:T(1,128)S(1)}, u32[]{:S(2)}, u32[]{:S(2)}) collective-permute-start(f32[20,18,1,128]{3,2,1,0:T(1,128)} %get-tuple-element.111), channel_id=1, source_target_pairs={{0,1},{1,2},{2,3},{3,4},{4,5},{5,6},{6,7},{7,8},{8,9},{9,10},{10,1... | collective-permute-start | bytes 552968 | tf_op jit(solution)/shard_map/ppermute | solution.py:46
  63.0 4.0 %bitcast_dynamic-update-slice_fusion.6 = (f32[20,16,32,128]{3,2,1,0:T(8,128)S(1)}, f32[16,32,128]{2,1,0:T(8,128)}, f32[16,32,128]{2,1,0:T(8,128)S(1)}, f32[16,32...) fusion(pred[16,32,128]{2,1,0:T(8,128)(4,1)S(1)} %get-tuple-elem, ...), kind=kLoop, calls=%fused_computation.699 | loop fusion | flops 9175039 | bytes 18653184
  71.1 2.3 copy-done.3
  73.6 3.6 %collective-permute-start.5 = (f32[20,1,32,128]{3,2,1,0:T(8,128)S(1)}, f32[20,1,32,128]{3,2,1,0:T(8,128)S(1)}, u32[]{:S(2)}, u32[]{:S(2)}) collective-permute-start(f32[20,1,32,128]{3,2,1,0:T(8,128)S(1)} %get-tuple-element.127), channel_id=1, source_target_pairs={{16,0},{32,16},{48,32},{64,48},{80,64},{96,80},{112,96},{0,112},{1... | collective-permute-start | bytes 983048 | tf_op jit(solution)/shard_map/ppermute | solution.py:48
  78.7 24.5 %collective-permute-done.4 = f32[20,1,32,128]{3,2,1,0:T(8,128)S(1)} collective-permute-done((f32[20,1,32,128]{3,2,1,0:T(8,128)S(1)}, f32[20,1,32,128]{3,2,1,0:T(8,128)S(1)}, u32[]{:S(2)}, u32[]{:S(2)}) %collective-permute-start.4) | collective-permute-done | bytes 327712 | tf_op jit(solution)/shard_map/ppermute | solution.py:46
  105.0 2.8 pad_maximum_fusion.67
  107.8 5.3 %collective-permute-start.6 = (f32[20,18,1,128]{3,2,1,0:T(1,128)}, f32[20,18,1,128]{3,2,1,0:T(1,128)S(1)}, u32[]{:S(2)}, u32[]{:S(2)}) collective-permute-start(f32[20,18,1,128]{3,2,1,0:T(1,128)} %get-tuple-element.107), channel_id=1, source_target_pairs={{0,1},{1,2},{2,3},{3,4},{4,5},{5,6},{6,7},{7,8},{8,9},{9,10},{10,1... | collective-permute-start | bytes 552968 | tf_op jit(solution)/shard_map/ppermute | solution.py:46
  113.1 6.3 %collective-permute-start.7 = (f32[20,18,1,128]{3,2,1,0:T(1,128)}, f32[20,18,1,128]{3,2,1,0:T(1,128)}, u32[]{:S(2)}, u32[]{:S(2)}) collective-permute-start(f32[20,18,1,128]{3,2,1,0:T(1,128)} %get-tuple-element.108), channel_id=1, source_target_pairs={{1,0},{2,1},{3,2},{4,3},{5,4},{6,5},{7,6},{8,7},{9,8},{10,9},{11,1... | collective-permute-start | bytes 552968 | tf_op jit(solution)/shard_map/ppermute | solution.py:48
  127.9 3.4 constant_dynamic-update-slice_fusion
  140.7 12.1 %collective-permute-done.8 = f32[20,1,32,128]{3,2,1,0:T(8,128)S(1)} collective-permute-done((f32[20,1,32,128]{3,2,1,0:T(8,128)S(1)}, f32[20,1,32,128]{3,2,1,0:T(8,128)S(1)}, u32[]{:S(2)}, u32[]{:S(2)}) %collective-permute-start.8) | collective-permute-done | bytes 327712 | tf_op jit(solution)/shard_map/ppermute | solution.py:46
  153.1 5.4 %collective-permute-start.11 = (f32[20,18,1,128]{3,2,1,0:T(1,128)S(1)}, f32[20,18,1,128]{3,2,1,0:T(1,128)S(1)}, u32[]{:S(2)}, u32[]{:S(2)}) collective-permute-start(f32[20,18,1,128]{3,2,1,0:T(1,128)S(1)} %get-tuple-element.103), channel_id=1, source_target_pairs={{1,0},{2,1},{3,2},{4,3},{5,4},{6,5},{7,6},{8,7},{9,8},{10,9},{11,1... | collective-permute-start | bytes 552968 | tf_op jit(solution)/shard_map/ppermute | solution.py:48
  160.7 23.0 %gather_fusion = f32[4096]{0:T(1024)S(1)} fusion(f32[65536]{0:T(1024)S(1)} %bitcast.598, s32[4096]{0:T(1024)S(1)} %copy-done.24), kind=kCustom, calls=%fused_computation | custom fusion | bytes 49152 | tf_op jit(solution)/shard_map/gather | solution.py:164
  183.8 23.0 %gather_fusion.1 = f32[4096]{0:T(1024)S(1)} fusion(f32[65536]{0:T(1024)S(1)} %bitcast.599, s32[4096]{0:T(1024)S(1)} %get-tuple-element.143), kind=kCustom, calls=%fused_computation.1 | custom fusion | bytes 49152 | tf_op jit(solution)/shard_map/gather | solution.py:188
  220.1 39.8 %psum.14 = f32[128]{0:T(128)S(1)} all-reduce(f32[128]{0:T(128)S(1)} %select_reduce_fusion), channel_id=1, replica_groups=mesh['slab'=8,'tile'=16] {'tile'}, use_global_device_ids=true, to_apply=%region_3.4 | all-reduce | flops 128 | bytes 1024 | tf_op jit(solution)/shard_map/psum | solution.py:165
  271.6 3.7 %fusion = f32[128,128]{1,0:T(8,128)S(1)} fusion(bf16[8,128,2048]{2,1,0:T(8,128)(2,1)} %all-gather.2.cloned.1.call-done, bf16[128,2048]{1,0:T(8,128)(2,1)S(1)} %copy-done, f32[128,8]{0,1:T(8,128)S(1)} %fusion.571), kind=kOutput, calls=%fused_computation.4 | convolution fusion | flops 537116672 | bytes 4788224 | tf_op jit(solution)/shard_map/dot_general | solution.py:168
  278.1 38.5 %psum.15 = f32[128]{0:T(128)S(1)} all-reduce(f32[128]{0:T(128)S(1)} %fusion.2), channel_id=1, replica_groups=mesh['slab'=8,'tile'=16] {'tile'}, use_global_device_ids=true, to_apply=%region_5.6 | all-reduce | flops 128 | bytes 1024 | tf_op jit(solution)/shard_map/psum | solution.py:185
  316.8 28.9 %scatter_fusion = f32[65536]{0:T(1024)S(1)} fusion(f32[65536]{0:T(1024)S(1)} %bitcast.600, s32[4096]{0:T(1024)S(1)} %bitcast.638, f32[4096]{0:T(1024)S(1)} %reshape.165), kind=kCustom, calls=%fused_computation.2 | custom fusion | flops 4096 | bytes 65536 | tf_op jit(solution)/shard_map/scatter-add | solution.py:190
  (243 shorter events, 74.5 us)
Async XLA Ops:
  7.2 112.2 %copy-start = (bf16[128,2048]{1,0:T(8,128)(2,1)S(1)}, bf16[128,2048]{1,0:T(8,128)(2,1)}, u32[]{:S(2)}) copy-start(bf16[128,2048]{1,0:T(8,128)(2,1)} %param.19) | copy-start | bytes 1572868
  7.2 264.4 %all-gather.2.cloned.1.call-start = ((), (), s32[]{:S(2)}) async-start(), calls=%async_computation | async-start | bytes 4718592 | tf_op jit(solution)/shard_map/all_gather | solution.py:166
  16.6 39.5 %copy-start.6 = (f32[16,32,128]{2,1,0:T(8,128)}, f32[16,32,128]{2,1,0:T(8,128)S(1)}, u32[]{:S(2)}) copy-start(f32[16,32,128]{2,1,0:T(8,128)S(1)} %get-tuple-element.80) | copy-start | bytes 786436
  16.8 38.4 %copy-start.10 = (f32[16,32,128]{2,1,0:T(8,128)}, f32[16,32,128]{2,1,0:T(8,128)S(1)}, u32[]{:S(2)}) copy-start(f32[16,32,128]{2,1,0:T(8,128)S(1)} %get-tuple-element.78) | copy-start | bytes 786436
  22.1 16.1 %collective-permute-start = (f32[20,1,32,128]{3,2,1,0:T(8,128)S(1)}, f32[20,1,32,128]{3,2,1,0:T(8,128)S(1)}, u32[]{:S(2)}, u32[]{:S(2)}) collective-permute-start(f32[20,1,32,128]{3,2,1,0:T(8,128)S(1)} %get-tuple-element.129), channel_id=1, source_target_pairs={{0,16},{16,32},{32,48},{48,64},{64,80},{80,96},{96,112},{112,0},{1... | collective-permute-start | bytes 983048 | tf_op jit(solution)/shard_map/ppermute | solution.py:46
  24.3 16.7 %collective-permute-start.1 = (f32[20,1,32,128]{3,2,1,0:T(8,128)S(1)}, f32[20,1,32,128]{3,2,1,0:T(8,128)S(1)}, u32[]{:S(2)}, u32[]{:S(2)}) collective-permute-start(f32[20,1,32,128]{3,2,1,0:T(8,128)S(1)} %get-tuple-element.130), channel_id=1, source_target_pairs={{16,0},{32,16},{48,32},{64,48},{80,64},{96,80},{112,96},{0,112},{1... | collective-permute-start | bytes 983048 | tf_op jit(solution)/shard_map/ppermute | solution.py:48
  41.0 19.0 %slice-start.4 = ((s8[5242880]{0:T(1024)(128)(4,1)}), s8[1048576]{0:T(1024)(128)(4,1)S(1)}, s32[]{:S(2)}) async-start(s8[5242880]{0:T(1024)(128)(4,1)} %bitcast.606), calls=%async_computation.5 | async-start | bytes 2097152
  43.9 15.5 %collective-permute-start.2 = (f32[20,18,1,128]{3,2,1,0:T(1,128)}, f32[20,18,1,128]{3,2,1,0:T(1,128)S(1)}, u32[]{:S(2)}, u32[]{:S(2)}) collective-permute-start(f32[20,18,1,128]{3,2,1,0:T(1,128)} %get-tuple-element.111), channel_id=1, source_target_pairs={{0,1},{1,2},{2,3},{3,4},{4,5},{5,6},{6,7},{7,8},{8,9},{9,10},{10,1... | collective-permute-start | bytes 552968 | tf_op jit(solution)/shard_map/ppermute | solution.py:46
  54.4 5.6 %collective-permute-start.3 = (f32[20,18,1,128]{3,2,1,0:T(1,128)}, f32[20,18,1,128]{3,2,1,0:T(1,128)}, u32[]{:S(2)}, u32[]{:S(2)}) collective-permute-start(f32[20,18,1,128]{3,2,1,0:T(1,128)} %get-tuple-element.112), channel_id=1, source_target_pairs={{1,0},{2,1},{3,2},{4,3},{5,4},{6,5},{7,6},{8,7},{9,8},{10,9},{11,1... | collective-permute-start | bytes 552968 | tf_op jit(solution)/shard_map/ppermute | solution.py:48
  68.2 54.2 %copy-start.8 = (f32[16,32,128]{2,1,0:T(8,128)}, f32[16,32,128]{2,1,0:T(8,128)S(1)}, u32[]{:S(2)}) copy-start(f32[16,32,128]{2,1,0:T(8,128)S(1)} %get-tuple-element.50) | copy-start | bytes 786436
  68.4 53.8 %copy-start.12 = (f32[16,32,128]{2,1,0:T(8,128)}, f32[16,32,128]{2,1,0:T(8,128)S(1)}, u32[]{:S(2)}) copy-start(f32[16,32,128]{2,1,0:T(8,128)S(1)} %get-tuple-element.48) | copy-start | bytes 786436
  73.5 29.7 %collective-permute-start.4 = (f32[20,1,32,128]{3,2,1,0:T(8,128)S(1)}, f32[20,1,32,128]{3,2,1,0:T(8,128)S(1)}, u32[]{:S(2)}, u32[]{:S(2)}) collective-permute-start(f32[20,1,32,128]{3,2,1,0:T(8,128)S(1)} %get-tuple-element.126), channel_id=1, source_target_pairs={{0,16},{16,32},{32,48},{48,64},{64,80},{80,96},{96,112},{112,0},{1... | collective-permute-start | bytes 983048 | tf_op jit(solution)/shard_map/ppermute | solution.py:46
  73.6 31.4 %collective-permute-start.5 = (f32[20,1,32,128]{3,2,1,0:T(8,128)S(1)}, f32[20,1,32,128]{3,2,1,0:T(8,128)S(1)}, u32[]{:S(2)}, u32[]{:S(2)}) collective-permute-start(f32[20,1,32,128]{3,2,1,0:T(8,128)S(1)} %get-tuple-element.127), channel_id=1, source_target_pairs={{16,0},{32,16},{48,32},{64,48},{80,64},{96,80},{112,96},{0,112},{1... | collective-permute-start | bytes 983048 | tf_op jit(solution)/shard_map/ppermute | solution.py:48
  107.8 16.5 %slice-start.2 = ((s8[5242880]{0:T(1024)(128)(4,1)}), s8[1048576]{0:T(1024)(128)(4,1)S(1)}, s32[]{:S(2)}) async-start(s8[5242880]{0:T(1024)(128)(4,1)} %bitcast.604), calls=%async_computation.3 | async-start | bytes 2097152
  107.8 16.5 %collective-permute-start.6 = (f32[20,18,1,128]{3,2,1,0:T(1,128)}, f32[20,18,1,128]{3,2,1,0:T(1,128)S(1)}, u32[]{:S(2)}, u32[]{:S(2)}) collective-permute-start(f32[20,18,1,128]{3,2,1,0:T(1,128)} %get-tuple-element.107), channel_id=1, source_target_pairs={{0,1},{1,2},{2,3},{3,4},{4,5},{5,6},{6,7},{7,8},{8,9},{9,10},{10,1... | collective-permute-start | bytes 552968 | tf_op jit(solution)/shard_map/ppermute | solution.py:46
  113.1 11.2 %collective-permute-start.7 = (f32[20,18,1,128]{3,2,1,0:T(1,128)}, f32[20,18,1,128]{3,2,1,0:T(1,128)}, u32[]{:S(2)}, u32[]{:S(2)}) collective-permute-start(f32[20,18,1,128]{3,2,1,0:T(1,128)} %get-tuple-element.108), channel_id=1, source_target_pairs={{1,0},{2,1},{3,2},{4,3},{5,4},{6,5},{7,6},{8,7},{9,8},{10,9},{11,1... | collective-permute-start | bytes 552968 | tf_op jit(solution)/shard_map/ppermute | solution.py:48
  135.3 24.7 %copy-start.2 = (f32[20,16,32,128]{3,2,1,0:T(8,128)}, f32[20,16,32,128]{3,2,1,0:T(8,128)S(1)}, u32[]{:S(2)}) copy-start(f32[20,16,32,128]{3,2,1,0:T(8,128)S(1)} %bitcast_dynamic-update-slice_fusion) | copy-start | bytes 15728644
  135.3 17.4 %collective-permute-start.8 = (f32[20,1,32,128]{3,2,1,0:T(8,128)S(1)}, f32[20,1,32,128]{3,2,1,0:T(8,128)S(1)}, u32[]{:S(2)}, u32[]{:S(2)}) collective-permute-start(f32[20,1,32,128]{3,2,1,0:T(8,128)S(1)} %get-tuple-element.124), channel_id=1, source_target_pairs={{0,16},{16,32},{32,48},{48,64},{64,80},{80,96},{96,112},{112,0},{1... | collective-permute-start | bytes 983048 | tf_op jit(solution)/shard_map/ppermute | solution.py:46
  137.5 15.2 %collective-permute-start.9 = (f32[20,1,32,128]{3,2,1,0:T(8,128)S(1)}, f32[20,1,32,128]{3,2,1,0:T(8,128)S(1)}, u32[]{:S(2)}, u32[]{:S(2)}) collective-permute-start(f32[20,1,32,128]{3,2,1,0:T(8,128)S(1)} %get-tuple-element.123), channel_id=1, source_target_pairs={{16,0},{32,16},{48,32},{64,48},{80,64},{96,80},{112,96},{0,112},{1... | collective-permute-start | bytes 983048 | tf_op jit(solution)/shard_map/ppermute | solution.py:48
  153.0 6.9 %collective-permute-start.10 = (f32[20,18,1,128]{3,2,1,0:T(1,128)S(1)}, f32[20,18,1,128]{3,2,1,0:T(1,128)S(1)}, u32[]{:S(2)}, u32[]{:S(2)}) collective-permute-start(f32[20,18,1,128]{3,2,1,0:T(1,128)S(1)} %get-tuple-element.104), channel_id=1, source_target_pairs={{0,1},{1,2},{2,3},{3,4},{4,5},{5,6},{6,7},{7,8},{8,9},{9,10},{10,1... | collective-permute-start | bytes 552968 | tf_op jit(solution)/shard_map/ppermute | solution.py:46
  153.1 6.9 %collective-permute-start.11 = (f32[20,18,1,128]{3,2,1,0:T(1,128)S(1)}, f32[20,18,1,128]{3,2,1,0:T(1,128)S(1)}, u32[]{:S(2)}, u32[]{:S(2)}) collective-permute-start(f32[20,18,1,128]{3,2,1,0:T(1,128)S(1)} %get-tuple-element.103), channel_id=1, source_target_pairs={{1,0},{2,1},{3,2},{4,3},{5,4},{6,5},{7,6},{8,7},{9,8},{10,9},{11,1... | collective-permute-start | bytes 552968 | tf_op jit(solution)/shard_map/ppermute | solution.py:48
  261.8 13.6 %copy-start.28 = (bf16[128,128]{0,1:T(8,128)(2,1)S(1)}, bf16[128,128]{0,1:T(8,128)(2,1)}, u32[]{:S(2)}) copy-start(bf16[128,128]{0,1:T(8,128)(2,1)} %copy.25) | copy-start | bytes 98308
  261.8 54.7 %copy-start.31 = (pred[128,32]{1,0:T(8,128)(4,1)S(1)}, pred[128,32]{1,0:T(8,128)(4,1)}, u32[]{:S(2)}) copy-start(pred[128,32]{1,0:T(8,128)(4,1)} %get-tuple-element.16) | copy-start | bytes 12292
  263.7 53.0 %copy-start.29 = (s32[4096,1]{0,1:T(1,128)S(1)}, s32[4096,1]{0,1:T(1,128)}, u32[]{:S(2)}) copy-start(s32[4096,1]{0,1:T(1,128)} %compare_select_fusion.2) | copy-start | bytes 49156
  (27 other events, 81.1 us)
Sparse Core Ops, SparseCore 0:
  26.7 112.7 all-gather.1
where the time goes:
time: 360 us; the launch traced here: 353 us
  other arithmetic  93.7 us (26%)
  blocking collectives  78.3 us (22%)
  local copies, waits for them, and re-layouts  70.2 us (20%)
  waiting for transfers between devices  51 us (14%)
  starting transfers between devices  39.4 us (11%)
  between operations  15 us (4%)
  matrix products  5.61 us (2%)
    ppermute x6, waiting for transfers between devices, extended(): lax.ppermute(tail, axis, [(i, (i + 1) % count) for i in range(count)])  45.8 us
    unnamed x75, other arithmetic  43.6 us
    psum x1, blocking collectives, per_device(): inlet_mean = lax.psum(partial_inlet, 'tile') / intake_face_position.shape[1]  39.8 us
    psum x1, blocking collectives, per_device(): exhaust = lax.psum(partial_exhaust, 'tile')  38.5 us
    scatter-add x1, other arithmetic, per_device(): flat_heat = flat_heat.at[exhaust_index.reshape(-1)].add(change.reshape(-1))  28.9 us
    gather x2, local copies, waits for them, and re-layouts, per_device(): flat_heat[inlet_index]  23.1 us
    gather x2, local copies, waits for them, and re-layouts, per_device(): old_values = flat_heat[exhaust_index]  23.1 us
    ppermute x6, starting transfers between devices, extended(): lax.ppermute(tail, axis, [(i, (i + 1) % count) for i in range(count)])  20.4 us
  transfers between devices with their start and end apart: 13, of which 6 were waited for; matrix products, arithmetic and copies ran while one was open for 33% of the time, Pallas kernels for 0%

commit v1 on v0

v1 whole, which is shorter than its diff:
```python
import functools

import jax
import jax.numpy as jnp
from jax import lax
from jax.experimental import pallas as pl
from jax.experimental.pallas import tpu as pltpu
from jax.sharding import PartitionSpec as P

MESH = pl.DeviceIdType.MESH
F32 = jnp.float32
BF16 = jnp.bfloat16

VELOCITY = (
    (0, 0, 0),
    (1, 0, 0),
    (-1, 0, 0),
    (0, 1, 0),
    (0, -1, 0),
    (0, 0, 1),
    (0, 0, -1),
    (1, 1, 0),
    (-1, -1, 0),
    (1, -1, 0),
    (-1, 1, 0),
    (1, 0, 1),
    (-1, 0, -1),
    (1, 0, -1),
    (-1, 0, 1),
    (0, 1, 1),
    (0, -1, -1),
    (0, 1, -1),
    (0, -1, 1),
)
X_UP = (1, 7, 9, 11, 13)
X_DOWN = (2, 8, 10, 12, 14)
Y_UP = (3, 7, 10, 15, 17)
Y_DOWN = (4, 8, 9, 16, 18)
CORNERS = ((7, 1, 1), (8, -1, -1), (9, 1, -1), (10, -1, 1))

relax_time = 0.6
buoyancy = 0.01
diffusion = 0.1
mixing = 0.5
keep_share = 0.5

NX, NY, NZ = 16, 32, 128
ROWS = 48
LOW, TOP = 7, 40
KINDS = 8
RACKS = 128
FACE = 32


def collide(f, heat, solid):
    omega = 1.0 / relax_time
    keep = 1.0 - omega
    even, odd = {}, {}
    for p in range(1, 19, 2):
        even[p] = f[p] + f[p + 1]
        odd[p] = f[p] - f[p + 1]
    density = (
        f[0]
        + ((even[1] + even[3]) + (even[5] + even[7]))
        + ((even[9] + even[11]) + (even[13] + even[15]))
        + even[17]
    )
    flow_x = (odd[1] + odd[7]) + (odd[9] + odd[11]) + odd[13]
    flow_y = (odd[3] + odd[7]) + (odd[15] - odd[9]) + odd[17]
    flow_z = (odd[5] + odd[11]) + (odd[15] - odd[13]) - odd[17]
    inverse = 1.0 / density
    ux = flow_x * inverse
    uy = flow_y * inverse
    uz = flow_z * inverse
    vz = uz + (relax_time * buoyancy) * heat * inverse
    rest = 1.0 - 1.5 * (ux * ux + uy * uy + vz * vz)
    share = density * (omega / 18.0)
    level = share * rest
    bend = share * 4.5
    lean = share * 3.0
    level_half, bend_half, lean_half = level * 0.5, bend * 0.5, lean * 0.5
    g = [None] * 19
    g[0] = jnp.where(solid, f[0], f[0] * keep + level * 6.0)
    along = {
        1: ux,
        3: uy,
        5: vz,
        7: ux + uy,
        9: ux - uy,
        11: ux + vz,
        13: ux - vz,
        15: uy + vz,
        17: uy - vz,
    }
    for p in range(1, 19, 2):
        c = along[p]
        lv, bd, ln = (level, bend, lean) if p < 7 else (level_half, bend_half, lean_half)
        same = lv + bd * (c * c)
        turn = ln * c
        g[p] = jnp.where(solid, f[p + 1], f[p] * keep + (same + turn))
        g[p + 1] = jnp.where(solid, f[p], f[p + 1] * keep + (same - turn))
    return g, (ux, uy, uz)


def shifted_z(v, step):
    return pltpu.roll(v, step % NZ, 1) if step else v


def face_masks(pos, slab, tile, tiles):
    pos = jnp.transpose(pos)
    height_bits = NZ.bit_length() - 1
    across = NY * tiles
    across_bits = across.bit_length() - 1
    px = jnp.right_shift(pos, height_bits + across_bits)
    py = jnp.bitwise_and(jnp.right_shift(pos, height_bits), across - 1)
    pz = jnp.bitwise_and(pos, NZ - 1)
    least = functools.partial(jnp.min, axis=0, keepdims=True)
    x0, y0, z0 = least(px), least(py), least(pz)
    y1 = jnp.max(py, axis=0, keepdims=True)
    lifted = least(py + jnp.where(py < across // 2, across, 0))
    y0 = jnp.where(y1 - y0 > 3, lifted, y0)
    row = lax.broadcasted_iota(jnp.int32, (NX * NY, RACKS), 0)
    gx = slab * NX + jnp.right_shift(row, 5)
    gy = tile * NY + jnp.bitwise_and(row, NY - 1)
    off_y = jnp.bitwise_and(gy - y0, across - 1)
    plan = jnp.where((gx == x0) & (off_y < 4), 1.0, 0.0).astype(F32)
    z = lax.broadcasted_iota(jnp.int32, (NZ, RACKS), 0)
    tall = jnp.where((z >= z0) & (z < z0 + 8), 1.0, 0.0).astype(F32)
    return plan, tall


def kernel(
    slabs,
    tiles,
    f_hbm,
    heat_hbm,
    solid_hbm,
    label_ref,
    inlet_hbm,
    outlet_hbm,
    matrix_ref,
    gain_ref,
    read_ref,
    state_ref,
    f_out,
    heat_out,
    states_out,
    fin,
    grid,
    warm,
    vel,
    solid_ref,
    inlet_ref,
    outlet_ref,
    x_send,
    x_recv,
    y_send,
    y_recv,
    c_recv,
    ty_send,
    ty_recv,
    kept,
    label_col,
    part,
    part_x,
    pair,
    part_y,
    base_ref,
    small_send,
    small_recv,
    load_sem,
    heat_sem,
    misc_sem,
    xs_sem,
    xr_sem,
    ys_sem,
    yr_sem,
    cs_sem,
    cr_sem,
    tsend_sem,
    trecv_sem,
    hs_sem,
    hr_sem,
    pxs_sem,
    pxr_sem,
    pys_sem,
    pyr_sem,
    ms_sem,
    mr_sem,
):
    slab = lax.axis_index("slab")
    tile = lax.axis_index("tile")
    s_up, s_down = lax.rem(slab + 1, slabs), lax.rem(slab + slabs - 1, slabs)
    t_up, t_down = lax.rem(tile + 1, tiles), lax.rem(tile + tiles - 1, tiles)
    core = lax.rem(tile, 2)
    partner = tile + 1 - 2 * core
    s_major = slab // 2
    s_minor = lax.rem(slab, 2)
    majors = slabs // 2

    def plane_copy(x):
        return pltpu.make_async_copy(f_hbm.at[:, x], fin.at[:, x], load_sem.at[x])

    def heat_copy(x):
        return pltpu.make_async_copy(
            heat_hbm.at[x], warm.at[0, x + 1, pl.ds(8, NY), :], heat_sem.at[x]
        )

    solid_copy = pltpu.make_async_copy(solid_hbm, solid_ref, misc_sem.at[0])
    first_rack = pl.multiple_of(slab * RACKS, RACKS)
    inlet_copy = pltpu.make_async_copy(
        inlet_hbm.at[pl.ds(first_rack, RACKS), :], inlet_ref, misc_sem.at[1]
    )
    outlet_copy = pltpu.make_async_copy(
        outlet_hbm.at[pl.ds(first_rack, RACKS), :], outlet_ref, misc_sem.at[2]
    )
    solid_copy.start()

    @pl.loop(0, NX)
    def _(x):
        heat_copy(x).start()

    plane_copy(0).start()
    plane_copy(NX - 1).start()

    @pl.loop(1, NX - 1)
    def _(x):
        plane_copy(x).start()

    inlet_copy.start()
    outlet_copy.start()

    barrier = pltpu.get_barrier_semaphore()

    @pl.loop(1, tiles)
    def _(d):
        pl.semaphore_signal(
            barrier, inc=1, device_id=(slab, lax.rem(tile + d, tiles)), device_id_type=MESH
        )

    @pl.loop(1, slabs)
    def _(d):
        pl.semaphore_signal(
            barrier, inc=1, device_id=(lax.rem(slab + d, slabs), tile), device_id_type=MESH
        )

    for ds in (s_up, s_down):
        for dt in (t_up, t_down):
            pl.semaphore_signal(barrier, inc=1, device_id=(ds, dt), device_id_type=MESH)

    def remote(src, dst, send, recv, to):
        return pltpu.make_async_remote_copy(
            src_ref=src,
            dst_ref=dst,
            send_sem=send,
            recv_sem=recv,
            device_id=to,
            device_id_type=MESH,
        )

    def x_copies(n):
        return [
            remote(x_send.at[n, 0], x_recv.at[n, 0], xs_sem.at[n, 0], xr_sem.at[n, 0], (s_up, tile)),
            remote(x_send.at[n, 1], x_recv.at[n, 1], xs_sem.at[n, 1], xr_sem.at[n, 1], (s_down, tile)),
        ]

    def y_copies(n):
        return [
            remote(y_send.at[n, 0], y_recv.at[n, 0], ys_sem.at[n, 0], yr_sem.at[n, 0], (slab, t_up)),
            remote(y_send.at[n, 1], y_recv.at[n, 1], ys_sem.at[n, 1], yr_sem.at[n, 1], (slab, t_down)),
        ]

    def c_copies(n):
        out = []
        for k, (lane, cx, cy) in enumerate(CORNERS):
            x = NX if cx > 0 else 1
            y = TOP - 8 if cy > 0 else LOW + 1
            to = (s_up if cx > 0 else s_down, t_up if cy > 0 else t_down)
            out.append(
                remote(
                    grid.at[n % 2, lane, x, pl.ds(y, 8), :],
                    c_recv.at[n, k],
                    cs_sem.at[n, k],
                    cr_sem.at[n, k],
                    to,
                )
            )
        return out

    def t_copies(n):
        own = pl.ds(8, NY)
        return [
            remote(
                warm.at[n, NX, own, :],
                warm.at[n, 0, own, :],
                tsend_sem.at[n, 0],
                trecv_sem.at[n, 0],
                (s_up, tile),
            ),
            remote(
                warm.at[n, 1, own, :],
                warm.at[n, NX + 1, own, :],
                tsend_sem.at[n, 1],
                trecv_sem.at[n, 1],
                (s_down, tile),
            ),
            remote(ty_send.at[n, 0], ty_recv.at[n, 0], tsend_sem.at[n, 2], trecv_sem.at[n, 2], (slab, t_up)),
            remote(ty_send.at[n, 1], ty_recv.at[n, 1], tsend_sem.at[n, 3], trecv_sem.at[n, 3], (slab, t_down)),
        ]

    def start_all(copies):
        for c in copies:
            c.start()

    def wait_recv_all(copies):
        for c in copies:
            c.wait_recv()

    def wait_send_all(copies):
        for c in copies:
            c.wait_send()

    def collide_block(n, x, yt):
        rows = pl.ds(8 + 8 * yt, 8)
        here = pl.ds(8 * yt, 8)
        if n == 0:
            f = [fin[i, x, here, :] for i in range(19)]
        else:
            old = (n - 1) % 2
            f = []
            for i, (cx, cy, cz) in enumerate(VELOCITY):
                v = grid[old, i, x + 1 - cx, pl.ds(8 + 8 * yt - cy, 8), :]
                f.append(shifted_z(v, cz))
        heat = warm[n, x + 1, rows, :]
        solid = solid_ref[x, here, :] == 1
        g, u = collide(f, heat, solid)
        new = n % 2
        for i in range(19):
            grid[new, i, x + 1, rows, :] = g[i]
        for d in range(3):
            vel[d, x, here, :] = u[d]

    def heat_block(n, x, yt):
        rows = pl.ds(8 + 8 * yt, 8)
        here = pl.ds(8 * yt, 8)
        centre = warm[n, x + 1, rows, :]
        pairs = (
            (warm[n, x, rows, :], warm[n, x + 2, rows, :]),
            (
                warm[n, x + 1, pl.ds(7 + 8 * yt, 8), :],
                warm[n, x + 1, pl.ds(9 + 8 * yt, 8), :],
            ),
            (shifted_z(centre, 1), shifted_z(centre, -1)),
        )
        laplace = -6.0 * centre
        carried = None
        for d in range(3):
            behind, ahead = pairs[d]
            laplace = laplace + (behind + ahead)
            term = vel[d, x, here, :] * (0.5 * (ahead - behind))
            carried = term if carried is None else carried + term
        solid = solid_ref[x, here, :] == 1
        warm[n + 1, x + 1, rows, :] = jnp.where(solid, centre, centre + diffusion * laplace - carried)

    def send_heat_rows(n):
        ty_send[n, 0] = warm[n, pl.ds(1, NX), TOP - 1, :]
        ty_send[n, 1] = warm[n, pl.ds(1, NX), LOW + 1, :]

    def take_heat_rows(n):
        warm[n, pl.ds(1, NX), LOW, :] = ty_recv[n, 0]
        warm[n, pl.ds(1, NX), TOP, :] = ty_recv[n, 1]

    def heat_pass(n):
        copies = t_copies(n)
        wait_recv_all(copies)
        take_heat_rows(n)

        @pl.loop(0, NX)
        def _(x):
            for yt in range(4):
                heat_block(n, x, yt)

        wait_send_all(copies)
        if n < 2:
            send_heat_rows(n + 1)
            start_all(t_copies(n + 1))

    def pack_x(n):
        own = pl.ds(8, NY)
        for k, lane in enumerate(X_UP):
            x_send[n, 0, k] = grid[n % 2, lane, NX, own, :].astype(BF16)
        for k, lane in enumerate(X_DOWN):
            x_send[n, 1, k] = grid[n % 2, lane, 1, own, :].astype(BF16)

    def pack_y(n):
        for k, lane in enumerate(Y_UP):
            y_send[n, 0, k] = grid[n % 2, lane, pl.ds(1, NX), TOP - 1, :].astype(BF16)
        for k, lane in enumerate(Y_DOWN):
            y_send[n, 1, k] = grid[n % 2, lane, pl.ds(1, NX), LOW + 1, :].astype(BF16)

    def take_all(n):
        wait_recv_all(x_copies(n))
        own = pl.ds(8, NY)
        for k, lane in enumerate(X_UP):
            grid[n % 2, lane, 0, own, :] = x_recv[n, 0, k].astype(F32)
        for k, lane in enumerate(X_DOWN):
            grid[n % 2, lane, NX + 1, own, :] = x_recv[n, 1, k].astype(F32)
        wait_recv_all(y_copies(n))
        for k, lane in enumerate(Y_UP):
            grid[n % 2, lane, pl.ds(1, NX), LOW, :] = y_recv[n, 0, k].astype(F32)
        for k, lane in enumerate(Y_DOWN):
            grid[n % 2, lane, pl.ds(1, NX), TOP, :] = y_recv[n, 1, k].astype(F32)
        wait_recv_all(c_copies(n))
        for k, (lane, cx, cy) in enumerate(CORNERS):
            x = 0 if cx > 0 else NX + 1
            y = LOW if cy > 0 else TOP
            row = 7 if cy > 0 else 0
            grid[n % 2, lane, x, pl.ds(y, 1), :] = c_recv[n, k, pl.ds(row, 1), :]

    def collide_pass(n, on_borders=None):
        @pl.loop(0, 2)
        def _(j):
            x = j * (NX - 1)
            if n == 0:
                plane_copy(x).wait()
            for yt in range(4):
                collide_block(n, x, yt)

        if on_borders is not None:
            on_borders()
        pack_x(n)
        start_all(x_copies(n))
        start_all(c_copies(n))

        @pl.loop(1, NX - 1)
        def _(x):
            if n == 0:
                plane_copy(x).wait()
            for yt in (0, 3):
                collide_block(n, x, yt)

        pack_y(n)
        start_all(y_copies(n))

        @pl.loop(1, NX - 1)
        def _(x):
            for yt in (1, 2):
                collide_block(n, x, yt)

    half_cols = 128
    my_half = pl.ds(pl.multiple_of(core * half_cols, half_cols), half_cols)

    def state_copy(d):
        to = lax.rem(slab + d, slabs)
        cols = pl.ds(pl.multiple_of(to * 256 + core * half_cols, half_cols), half_cols)
        return remote(
            state_ref.at[:, cols],
            kept.at[slab, :, my_half],
            hs_sem.at[d],
            hr_sem.at[d],
            (to, tile),
        )

    def partner_copy():
        return remote(
            kept.at[:, :, my_half],
            kept.at[:, :, my_half],
            hs_sem.at[0],
            hr_sem.at[0],
            (slab, partner),
        )

    def start_states():
        for d in range(1, slabs):
            state_copy(d).start()
        mine = pl.ds(pl.multiple_of(slab * 256 + core * half_cols, half_cols), half_cols)
        kept[slab, :, my_half] = state_ref[:, mine]

    def share_states():
        for d in range(1, slabs):
            state_copy(d).wait()
        partner_copy().start()

    def major_copy(d):
        to = lax.rem(s_major + d, majors)
        return remote(
            part.at[pl.ds(2 * to, 2)],
            part_x.at[d - 1],
            pxs_sem.at[d - 1],
            pxr_sem.at[d - 1],
            (2 * to + s_minor, tile),
        )

    def minor_copy():
        return remote(
            pair.at[1 - s_minor],
            part_y,
            pys_sem.at[0],
            pyr_sem.at[0],
            (2 * s_major + 1 - s_minor, tile),
        )

    def multiply():
        partner_copy().wait()

        @pl.loop(0, slabs)
        def _(b):
            labels = label_ref[pl.ds(b, 1), :]
            column = jnp.transpose(jnp.broadcast_to(labels, (RACKS, 128)))
            block = kept[b]
            total = jnp.zeros((RACKS, 128), F32)
            for k2 in range(KINDS // 2):
                weights = matrix_ref[pl.ds(2 * k2, 2)].reshape(256, 256)
                product = lax.dot_general(
                    block, weights, (((1,), (1,)), ((), ())), preferred_element_type=F32
                )
                total = jnp.where(column == 2 * k2, product[:, :128], total)
                total = jnp.where(column == 2 * k2 + 1, product[:, 128:], total)
            part[b] = total

        for d in range(1, majors):
            major_copy(d).start()

    def reduce_major():
        for d in range(1, majors):
            major_copy(d).wait()
        pair[...] = ((part[pl.ds(2 * s_major, 2)] + part_x[0]) + part_x[1]) + part_x[2]
        minor_copy().start()

    def finish_states():
        labels = label_ref[pl.ds(slab, 1), :]
        column = jnp.transpose(jnp.broadcast_to(labels, (RACKS, 128)))
        label_col[...] = column
        minor_copy().wait()
        cols = pl.ds(pl.multiple_of(tile * 128, 128), 128)
        base = keep_share * state_ref[:, cols].astype(F32) + (pair[s_minor] + part_y[...])
        base_ref[...] = base
        read = jnp.zeros((RACKS, 128), F32)
        for k in range(KINDS):
            read = jnp.where(column == k, read_ref[k : k + 1, cols], read)
        return jnp.sum(jnp.transpose(read * base), axis=0, keepdims=True)

    def small_copy(d):
        return remote(
            small_send,
            small_recv.at[d],
            ms_sem.at[d],
            mr_sem.at[d],
            (slab, lax.rem(tile + d, tiles)),
        )

    def after_first_borders():
        pl.semaphore_wait(barrier, (tiles - 1) + (slabs - 1) + 4)
        send_heat_rows(0)
        start_all(t_copies(0))

    solid_copy.wait()

    @pl.loop(0, NX)
    def _(x):
        heat_copy(x).wait()

    collide_pass(0, after_first_borders)
    start_states()
    heat_pass(0)
    take_all(0)
    wait_send_all(x_copies(0) + y_copies(0) + c_copies(0))

    collide_pass(1)
    share_states()
    heat_pass(1)
    multiply()
    take_all(1)
    wait_send_all(x_copies(1) + y_copies(1) + c_copies(1))

    collide_pass(2)
    heat_pass(2)

    inlet_copy.wait()
    outlet_copy.wait()
    plan, tall = face_masks(inlet_ref[...], slab, tile, tiles)
    final = warm[3, pl.ds(1, NX), pl.ds(8, NY), :].reshape(NX * NY, NZ)
    sums = jnp.dot(final, tall, precision=lax.Precision.HIGHEST, preferred_element_type=F32)
    inlet_part = jnp.sum(plan * sums, axis=0, keepdims=True)
    reduce_major()
    read_part = finish_states()
    small_send[pl.ds(0, 1), :] = inlet_part
    small_send[pl.ds(1, 1), :] = read_part
    small_send[pl.ds(2, 6), :] = jnp.zeros((6, 128), F32)

    for d in range(1, tiles):
        small_copy(d).start()

    take_all(2)

    @pl.loop(0, NX)
    def _(x):
        for i, (cx, cy, cz) in enumerate(VELOCITY):
            v = grid[0, i, x + 1 - cx, pl.ds(8 - cy, NY), :]
            f_out[i, x] = shifted_z(v, cz)

    wait_send_all(x_copies(2) + y_copies(2) + c_copies(2))

    column = label_col[...]
    cols = pl.ds(pl.multiple_of(tile * 128, 128), 128)
    gain = jnp.zeros((RACKS, 128), F32)
    for k in range(KINDS):
        gain = jnp.where(column == k, gain_ref[k : k + 1, cols], gain)
    response = jnp.sum(gain_ref[...] * read_ref[...], axis=1, keepdims=True)
    kinds = lax.broadcasted_iota(jnp.int32, (KINDS, 128), 0)
    labels = label_ref[pl.ds(slab, 1), :]
    response_row = jnp.sum(jnp.where(kinds == labels, response, 0.0), axis=0, keepdims=True)
    plan, tall = face_masks(outlet_ref[...], slab, tile, tiles)

    for d in range(1, tiles):
        small_copy(d).wait()
    total = small_send[...]
    for d in range(1, tiles):
        total = total + small_recv[d]
    inlet = total[0:1, :] * (1.0 / FACE)
    exhaust = total[1:2, :] + response_row * inlet
    states_out[...] = base_ref[...] + gain * jnp.transpose(jnp.broadcast_to(inlet, (128, RACKS)))
    dims = (((1,), (1,)), ((), ()))
    spread = lax.dot_general(
        plan * exhaust, tall, dims, precision=lax.Precision.HIGHEST, preferred_element_type=F32
    )
    inside = lax.dot_general(
        plan.astype(BF16), tall.astype(BF16), dims, preferred_element_type=F32
    )
    final = warm[3, pl.ds(1, NX), pl.ds(8, NY), :].reshape(NX * NY, NZ)
    result = final + mixing * (spread - inside * final)
    heat_out[...] = result.reshape(NX, NY, NZ)


def per_device(slabs, tiles, f, heat, solid, label, inlet, outlet, matrix, gain, read, state):
    vmem = pl.BlockSpec(memory_space=pltpu.VMEM)
    hbm = pl.BlockSpec(memory_space=pl.ANY)
    dma = pltpu.SemaphoreType.DMA
    return pl.pallas_call(
        functools.partial(kernel, slabs, tiles),
        out_shape=(
            jax.ShapeDtypeStruct((19, NX, NY, NZ), F32),
            jax.ShapeDtypeStruct((NX, NY, NZ), F32),
            jax.ShapeDtypeStruct((RACKS, 128), F32),
        ),
        in_specs=[hbm, hbm, hbm, vmem, hbm, hbm, vmem, vmem, vmem, vmem],
        out_specs=(vmem, vmem, vmem),
        scratch_shapes=[
            pltpu.VMEM((19, NX, NY, NZ), F32),
            pltpu.VMEM((2, 19, NX + 2, ROWS, NZ), F32),
            pltpu.VMEM((4, NX + 2, ROWS, NZ), F32),
            pltpu.VMEM((3, NX, NY, NZ), F32),
            pltpu.VMEM((NX, NY, NZ), jnp.int32),
            pltpu.VMEM((RACKS, FACE), jnp.int32),
            pltpu.VMEM((RACKS, FACE), jnp.int32),
            pltpu.VMEM((3, 2, 5, NY, NZ), BF16),
            pltpu.VMEM((3, 2, 5, NY, NZ), BF16),
            pltpu.VMEM((3, 2, 5, NX, NZ), BF16),
            pltpu.VMEM((3, 2, 5, NX, NZ), BF16),
            pltpu.VMEM((3, 4, 8, NZ), F32),
            pltpu.VMEM((3, 2, NX, NZ), F32),
            pltpu.VMEM((3, 2, NX, NZ), F32),
            pltpu.VMEM((slabs, RACKS, 256), BF16),
            pltpu.VMEM((RACKS, 128), jnp.int32),
            pltpu.VMEM((slabs, RACKS, 128), F32),
            pltpu.VMEM((slabs // 2 - 1, 2, RACKS, 128), F32),
            pltpu.VMEM((2, RACKS, 128), F32),
            pltpu.VMEM((RACKS, 128), F32),
            pltpu.VMEM((RACKS, 128), F32),
            pltpu.VMEM((8, 128), F32),
            pltpu.VMEM((tiles, 8, 128), F32),
            dma((NX,)),
            dma((NX,)),
            dma((3,)),
            dma((3, 2)),
            dma((3, 2)),
            dma((3, 2)),
            dma((3, 2)),
            dma((3, 4)),
            dma((3, 4)),
            dma((3, 4)),
            dma((3, 4)),
            dma((slabs,)),
            dma((slabs,)),
            dma((3,)),
            dma((3,)),
            dma((1,)),
            dma((1,)),
            dma((tiles,)),
            dma((tiles,)),
        ],
        compiler_params=pltpu.CompilerParams(
            collective_id=0, has_side_effects=True, vmem_limit_bytes=56 * 1024 * 1024
        ),
    )(f, heat, solid, label.reshape(8, 128), inlet, outlet, matrix, gain, read, state)


def solution(mesh):
    slabs, tiles = mesh.shape["slab"], mesh.shape["tile"]
    return jax.shard_map(
        functools.partial(per_device, slabs, tiles),
        mesh=mesh,
        in_specs=(
            P(None, "slab", "tile", None),
            P("slab", "tile", None),
            P("slab", "tile", None),
            P(),
            P(),
            P(),
            P(None, "tile", "slab"),
            P(),
            P(),
            P("slab", None),
        ),
        out_specs=(P(None, "slab", "tile", None), P("slab", "tile", None), P("slab", "tile")),
        check_vma=False,
    )
```

time: 360 us -> 60.2 us (0.17); the launches traced: 353 us -> 60.1 us
  other arithmetic: 93.7 us -> 0 us
  blocking collectives: 78.3 us -> 0 us
  local copies, waits for them, and re-layouts: 70.2 us -> 10.6 us
  waiting for transfers between devices: 51 us -> 0 us
  Pallas kernels: 0 us -> 48.8 us
  starting transfers between devices: 39.4 us -> 0 us
  between operations: 15 us -> 0.66 us
  matrix products: 5.61 us -> 0 us
    psum x2 -> x0, blocking collectives: 78.3 us -> none  [the longest x1 39.8 us: per_device(): inlet_mean = lax.psum(partial_inlet, 'tile') / intake_face_position.shape[1]]
    ppermute x12 -> x0, waiting for transfers between devices: 51 us -> none  [the longest x6 45.8 us: extended(): lax.ppermute(tail, axis, [(i, (i + 1) % count) for i in range(count)])]
    pallas_call x0 -> x1, Pallas kernels: none -> 48.8 us  [per_device(): pl.pallas_call(functools.partial(kernel, slabs, tiles), out_shape=(jax.Sh...]
    gather x4 -> x0, local copies, waits for them, and re-layouts: 46.2 us -> none  [the longest x2 23.1 us: per_device(): flat_heat[inlet_index]]
    unnamed x75 -> x0, other arithmetic: 43.6 us -> none
    ppermute x12 -> x0, starting transfers between devices: 39.3 us -> none  [the longest x6 20.4 us: extended(): lax.ppermute(tail, axis, [(i, (i + 1) % count) for i in range(count)])]
    scatter-add x1 -> x0, other arithmetic: 28.9 us -> none  [per_device(): flat_heat = flat_heat.at[exhaust_index.reshape(-1)].add(change.reshape(-1))]
    slice x39 -> x0, local copies, waits for them, and re-layouts: 10.5 us -> none  [the longest x30 9.5 us: advance(): passed.append(jnp.roll(moved, stride[2], axis=2))]
  transfers between devices with their start and end apart: 13 -> 0, of which waited for: 6 -> 0; matrix products, arithmetic and copies ran while one was open for 33% -> 0% of each run, Pallas kernels for 0% -> 0%
where the time goes in v1:
time: 60.2 us; the launch traced here: 60.1 us
  Pallas kernels  48.8 us (81%)
  local copies, waits for them, and re-layouts  10.6 us (18%)
  between operations  0.66 us (1%)
    pallas_call x1, Pallas kernels, per_device(): pl.pallas_call(functools.partial(kernel, slabs, tiles), out_shape=(jax.Sh...  48.8 us
    unnamed x9, local copies, waits for them, and re-layouts  10.6 us

profile of v1, /device:TPU:1, one launch (start us, length us, event | category | flops | bytes accessed | tf_op | source)
XLA Modules:
  0.0 60.1 jit_solution(8844916077237472095)
XLA Ops:
  0.6 1.9 %copy.13.inlet_hbm = s32[1024,32]{1,0:T(8,128)} copy(s32[1024,32]{0,1:T(8,128)} %param.14) | data formatting | bytes 262144 | tf_op args[4]
  2.5 1.9 %copy.14.outlet_hbm = s32[1024,32]{1,0:T(8,128)} copy(s32[1024,32]{0,1:T(8,128)} %param.15) | data formatting | bytes 262144 | tf_op args[5]
  4.4 48.8 %shard_map.121 = (f32[19,16,32,128]{3,2,1,0:T(8,128)}, f32[16,32,128]{2,1,0:T(8,128)}, f32[128,128]{1,0:T(8,128)}) custom-call(f32[19,16,32,128]{3,2,1,0:T(8,128)} %f_hbm.1, f32[16,32,128]{2,1,0:T(8,128)} %heat_hbm.1, s32[16,32,128]{2,1,0:T(8,128)} %solid_hbm.1, s32[8,128]{1,0:T(8,128)} %bitcast.1, s32[1024,32]{1,0:T(8,128)} %copy.13.inlet_hbm, ...), custom_call_target="tpu_custom_call" | custom-call | tf_op jit(solution)/shard_map/pallas_call | solution.py:639
  53.2 0.0 copy-start
  53.2 0.0 copy-start.1
  53.2 5.5 %copy.18 = f32[19,16,32,128]{3,2,1,0:T(8,128)} copy(f32[19,16,32,128]{3,2,1,0:T(8,128)} %get-tuple-element.6) | data formatting | bytes 9961472
  58.7 0.0 copy-done
  58.7 0.7 %copy.19 = f32[16,32,128]{2,1,0:T(8,128)} copy(f32[16,32,128]{2,1,0:T(8,128)S(1)} %copy-done) | data formatting | bytes 524288
  59.4 0.0 copy-done.1
  59.4 0.6 %copy.20 = f32[128,128]{1,0:T(8,128)} copy(f32[128,128]{1,0:T(8,128)S(1)} %copy-done.1) | data formatting | bytes 131072
Async XLA Ops:
  53.2 5.5 %copy-start = (f32[16,32,128]{2,1,0:T(8,128)S(1)}, f32[16,32,128]{2,1,0:T(8,128)}, u32[]{:S(2)}) copy-start(f32[16,32,128]{2,1,0:T(8,128)} %get-tuple-element.7) | copy-start | bytes 786436
  53.2 6.2 %copy-start.1 = (f32[128,128]{1,0:T(8,128)S(1)}, f32[128,128]{1,0:T(8,128)}, u32[]{:S(2)}) copy-start(f32[128,128]{1,0:T(8,128)} %get-tuple-element.8) | copy-start | bytes 196612

commit v2 on v1

--- a/solution.py
+++ b/solution.py
@@ -68,37 +68,43 @@
     flow_x = (odd[1] + odd[7]) + (odd[9] + odd[11]) + odd[13]
     flow_y = (odd[3] + odd[7]) + (odd[15] - odd[9]) + odd[17]
     flow_z = (odd[5] + odd[11]) + (odd[15] - odd[13]) - odd[17]
-    inverse = 1.0 / density
+    inverse = jnp.where(solid, 0.0, 1.0 / density)
+    share = jnp.where(solid, 0.0, density * (omega / 18.0))
+    even_part = jnp.where(solid, 0.5, 0.5 * keep)
+    odd_part = jnp.where(solid, -0.5, 0.5 * keep)
     ux = flow_x * inverse
     uy = flow_y * inverse
     uz = flow_z * inverse
-    vz = uz + (relax_time * buoyancy) * heat * inverse
-    rest = 1.0 - 1.5 * (ux * ux + uy * uy + vz * vz)
-    share = density * (omega / 18.0)
-    level = share * rest
+    vz = (flow_z + (relax_time * buoyancy) * heat) * inverse
     bend = share * 4.5
     lean = share * 3.0
-    level_half, bend_half, lean_half = level * 0.5, bend * 0.5, lean * 0.5
+    ex, ey, ez = bend * ux, bend * uy, bend * vz
+    xx, yy, zz = ex * ux, ey * uy, ez * vz
+    level = share - (xx + yy + zz) * (1.0 / 3.0)
+    sx, sy, sz = level + xx, level + yy, level + zz
+    tx, ty, tz = lean * ux, lean * uy, lean * vz
+    hx, hy, hz = 0.5 * tx, 0.5 * ty, 0.5 * tz
+    mxy, mxz, myz = 0.5 * (sx + yy), 0.5 * (sx + zz), 0.5 * (sy + zz)
+    qxy, qxz, qyz = ex * uy, ex * vz, ey * vz
+    terms = {
+        1: (sx, tx),
+        3: (sy, ty),
+        5: (sz, tz),
+        7: (mxy + qxy, hx + hy),
+        9: (mxy - qxy, hx - hy),
+        11: (mxz + qxz, hx + hz),
+        13: (mxz - qxz, hx - hz),
+        15: (myz + qyz, hy + hz),
+        17: (myz - qyz, hy - hz),
+    }
     g = [None] * 19
-    g[0] = jnp.where(solid, f[0], f[0] * keep + level * 6.0)
-    along = {
-        1: ux,
-        3: uy,
-        5: vz,
-        7: ux + uy,
-        9: ux - uy,
-        11: ux + vz,
-        13: ux - vz,
-        15: uy + vz,
-        17: uy - vz,
-    }
+    g[0] = f[0] * jnp.where(solid, 1.0, keep) + level * 6.0
     for p in range(1, 19, 2):
-        c = along[p]
-        lv, bd, ln = (level, bend, lean) if p < 7 else (level_half, bend_half, lean_half)
-        same = lv + bd * (c * c)
-        turn = ln * c
-        g[p] = jnp.where(solid, f[p + 1], f[p] * keep + (same + turn))
-        g[p + 1] = jnp.where(solid, f[p], f[p + 1] * keep + (same - turn))
+        same, turn = terms[p]
+        both = even[p] * even_part + same
+        half = odd[p] * odd_part + turn
+        g[p] = both + half
+        g[p + 1] = both - half
     return g, (ux, uy, uz)
 
 
@@ -107,7 +113,6 @@
 
 
 def face_masks(pos, slab, tile, tiles):
-    pos = jnp.transpose(pos)
     height_bits = NZ.bit_length() - 1
     across = NY * tiles
     across_bits = across.bit_length() - 1
@@ -123,10 +128,17 @@
     gx = slab * NX + jnp.right_shift(row, 5)
     gy = tile * NY + jnp.bitwise_and(row, NY - 1)
     off_y = jnp.bitwise_and(gy - y0, across - 1)
-    plan = jnp.where((gx == x0) & (off_y < 4), 1.0, 0.0).astype(F32)
+    plan = jnp.where((gx == x0) & (off_y < 4), 1.0, 0.0).astype(BF16)
     z = lax.broadcasted_iota(jnp.int32, (NZ, RACKS), 0)
-    tall = jnp.where((z >= z0) & (z < z0 + 8), 1.0, 0.0).astype(F32)
+    tall = jnp.where((z >= z0) & (z < z0 + 8), 1.0, 0.0).astype(BF16)
     return plan, tall
+
+
+def three_parts(v):
+    a = v.astype(BF16)
+    rest = v - a.astype(F32)
+    b = rest.astype(BF16)
+    return a, b, (rest - b.astype(F32)).astype(BF16)
 
 
 def kernel(
@@ -135,13 +147,13 @@
     f_hbm,
     heat_hbm,
     solid_hbm,
-    label_ref,
+    label_hbm,
     inlet_hbm,
     outlet_hbm,
-    matrix_ref,
-    gain_ref,
-    read_ref,
-    state_ref,
+    matrix_hbm,
+    gain_hbm,
+    read_hbm,
+    state_hbm,
     f_out,
     heat_out,
     states_out,
@@ -152,6 +164,11 @@
     solid_ref,
     inlet_ref,
     outlet_ref,
+    label_ref,
+    matrix_ref,
+    gain_ref,
+    read_ref,
+    state_ref,
     x_send,
     x_recv,
     y_send,
@@ -161,6 +178,13 @@
     ty_recv,
     kept,
     label_col,
+    plan_in,
+    tall_in,
+    plan_out,
+    tall_out,
+    gain_rows,
+    read_rows,
+    response,
     part,
     part_x,
     pair,
@@ -209,10 +233,10 @@
     solid_copy = pltpu.make_async_copy(solid_hbm, solid_ref, misc_sem.at[0])
     first_rack = pl.multiple_of(slab * RACKS, RACKS)
     inlet_copy = pltpu.make_async_copy(
-        inlet_hbm.at[pl.ds(first_rack, RACKS), :], inlet_ref, misc_sem.at[1]
+        inlet_hbm.at[:, pl.ds(first_rack, RACKS)], inlet_ref, misc_sem.at[1]
     )
     outlet_copy = pltpu.make_async_copy(
-        outlet_hbm.at[pl.ds(first_rack, RACKS), :], outlet_ref, misc_sem.at[2]
+        outlet_hbm.at[:, pl.ds(first_rack, RACKS)], outlet_ref, misc_sem.at[2]
     )
     solid_copy.start()
 
@@ -227,8 +251,15 @@
     def _(x):
         plane_copy(x).start()
 
-    inlet_copy.start()
-    outlet_copy.start()
+    label_copy = pltpu.make_async_copy(label_hbm, label_ref, misc_sem.at[3])
+    matrix_copy = pltpu.make_async_copy(matrix_hbm, matrix_ref, misc_sem.at[4])
+    gain_copy = pltpu.make_async_copy(gain_hbm, gain_ref, misc_sem.at[5])
+    read_copy = pltpu.make_async_copy(read_hbm, read_ref, misc_sem.at[6])
+    state_copy_in = pltpu.make_async_copy(state_hbm, state_ref, misc_sem.at[7])
+    state_copy_in.start()
+    table_copies = (label_copy, inlet_copy, outlet_copy, gain_copy, read_copy, matrix_copy)
+    for c in table_copies:
+        c.start()
 
     barrier = pltpu.get_barrier_semaphore()
 
@@ -417,7 +448,7 @@
             row = 7 if cy > 0 else 0
             grid[n % 2, lane, x, pl.ds(y, 1), :] = c_recv[n, k, pl.ds(row, 1), :]
 
-    def collide_pass(n, on_borders=None):
+    def edges(n):
         @pl.loop(0, 2)
         def _(j):
             x = j * (NX - 1)
@@ -426,12 +457,7 @@
             for yt in range(4):
                 collide_block(n, x, yt)
 
-        if on_borders is not None:
-            on_borders()
-        pack_x(n)
-        start_all(x_copies(n))
-        start_all(c_copies(n))
-
+    def rims(n):
         @pl.loop(1, NX - 1)
         def _(x):
             if n == 0:
@@ -439,13 +465,20 @@
             for yt in (0, 3):
                 collide_block(n, x, yt)
 
-        pack_y(n)
-        start_all(y_copies(n))
-
+    def middle(n):
         @pl.loop(1, NX - 1)
         def _(x):
             for yt in (1, 2):
                 collide_block(n, x, yt)
+
+    def send_x(n):
+        pack_x(n)
+        start_all(x_copies(n))
+        start_all(c_copies(n))
+
+    def send_y(n):
+        pack_y(n)
+        start_all(y_copies(n))
 
     half_cols = 128
     my_half = pl.ds(pl.multiple_of(core * half_cols, half_cols), half_cols)
@@ -503,12 +536,13 @@
     def multiply():
         partner_copy().wait()
 
-        @pl.loop(0, slabs)
-        def _(b):
-            labels = label_ref[pl.ds(b, 1), :]
-            column = jnp.transpose(jnp.broadcast_to(labels, (RACKS, 128)))
-            block = kept[b]
-            total = jnp.zeros((RACKS, 128), F32)
+        rows = 256
+
+        @pl.loop(0, slabs * RACKS // rows)
+        def _(m):
+            block = kept[pl.ds(2 * m, 2)].reshape(rows, 256)
+            column = label_col[pl.ds(pl.multiple_of(m * rows, rows), rows), :]
+            total = jnp.zeros((rows, 128), F32)
             for k2 in range(KINDS // 2):
                 weights = matrix_ref[pl.ds(2 * k2, 2)].reshape(256, 256)
                 product = lax.dot_general(
@@ -516,7 +550,7 @@
                 )
                 total = jnp.where(column == 2 * k2, product[:, :128], total)
                 total = jnp.where(column == 2 * k2 + 1, product[:, 128:], total)
-            part[b] = total
+            part[pl.ds(2 * m, 2)] = total.reshape(2, RACKS, 128)
 
         for d in range(1, majors):
             major_copy(d).start()
@@ -527,18 +561,39 @@
         pair[...] = ((part[pl.ds(2 * s_major, 2)] + part_x[0]) + part_x[1]) + part_x[2]
         minor_copy().start()
 
+    def tables():
+        for c in table_copies:
+            c.wait()
+        plan_in[...], tall_in[...] = face_masks(inlet_ref[...], slab, tile, tiles)
+        plan_out[...], tall_out[...] = face_masks(outlet_ref[...], slab, tile, tiles)
+
+        @pl.loop(0, slabs)
+        def _(b):
+            labels = label_ref[pl.ds(b, 1), :]
+            rows = pl.ds(pl.multiple_of(b * RACKS, RACKS), RACKS)
+            label_col[rows, :] = jnp.transpose(jnp.broadcast_to(labels, (RACKS, 128)))
+
+        column = label_col[pl.ds(first_rack, RACKS), :]
+        cols = pl.ds(pl.multiple_of(tile * 128, 128), 128)
+        gain = jnp.zeros((RACKS, 128), F32)
+        read = jnp.zeros((RACKS, 128), F32)
+        for k in range(KINDS):
+            gain = jnp.where(column == k, gain_ref[k : k + 1, cols], gain)
+            read = jnp.where(column == k, read_ref[k : k + 1, cols], read)
+        gain_rows[...] = gain
+        read_rows[...] = read
+        per_kind = jnp.sum(gain_ref[...] * read_ref[...], axis=1, keepdims=True)
+        kinds = lax.broadcasted_iota(jnp.int32, (KINDS, 128), 0)
+        labels = label_ref[pl.ds(slab, 1), :]
+        row = jnp.sum(jnp.where(kinds == labels, per_kind, 0.0), axis=0, keepdims=True)
+        response[...] = jnp.broadcast_to(row, (8, 128))
+
     def finish_states():
-        labels = label_ref[pl.ds(slab, 1), :]
-        column = jnp.transpose(jnp.broadcast_to(labels, (RACKS, 128)))
-        label_col[...] = column
         minor_copy().wait()
         cols = pl.ds(pl.multiple_of(tile * 128, 128), 128)
         base = keep_share * state_ref[:, cols].astype(F32) + (pair[s_minor] + part_y[...])
         base_ref[...] = base
-        read = jnp.zeros((RACKS, 128), F32)
-        for k in range(KINDS):
-            read = jnp.where(column == k, read_ref[k : k + 1, cols], read)
-        return jnp.sum(jnp.transpose(read * base), axis=0, keepdims=True)
+        return jnp.sum(jnp.transpose(read_rows[...] * base), axis=0, keepdims=True)
 
     def small_copy(d):
         return remote(
@@ -549,10 +604,10 @@
             (slab, lax.rem(tile + d, tiles)),
         )
 
-    def after_first_borders():
-        pl.semaphore_wait(barrier, (tiles - 1) + (slabs - 1) + 4)
-        send_heat_rows(0)
-        start_all(t_copies(0))
+    def stream_plane(x):
+        for i, (cx, cy, cz) in enumerate(VELOCITY):
+            v = grid[0, i, x + 1 - cx, pl.ds(8 - cy, NY), :]
+            f_out[i, x] = shifted_z(v, cz)
 
     solid_copy.wait()
 
@@ -560,29 +615,45 @@
     def _(x):
         heat_copy(x).wait()
 
-    collide_pass(0, after_first_borders)
+    edges(0)
+    rims(0)
+    pl.semaphore_wait(barrier, (tiles - 1) + (slabs - 1) + 4)
+    send_heat_rows(0)
+    start_all(t_copies(0))
+    send_x(0)
+    send_y(0)
+    state_copy_in.wait()
     start_states()
+    middle(0)
+    tables()
     heat_pass(0)
+    share_states()
     take_all(0)
     wait_send_all(x_copies(0) + y_copies(0) + c_copies(0))
 
-    collide_pass(1)
-    share_states()
+    edges(1)
+    send_x(1)
+    rims(1)
+    send_y(1)
+    multiply()
+    middle(1)
     heat_pass(1)
-    multiply()
     take_all(1)
     wait_send_all(x_copies(1) + y_copies(1) + c_copies(1))
 
-    collide_pass(2)
+    edges(2)
+    send_x(2)
+    rims(2)
+    send_y(2)
+    reduce_major()
+    middle(2)
     heat_pass(2)
 
-    inlet_copy.wait()
-    outlet_copy.wait()
-    plan, tall = face_masks(inlet_ref[...], slab, tile, tiles)
     final = warm[3, pl.ds(1, NX), pl.ds(8, NY), :].reshape(NX * NY, NZ)
-    sums = jnp.dot(final, tall, precision=lax.Precision.HIGHEST, preferred_element_type=F32)
-    inlet_part = jnp.sum(plan * sums, axis=0, keepdims=True)
-    reduce_major()
+    sums = jnp.zeros((NX * NY, RACKS), F32)
+    for piece in three_parts(final):
+        sums = sums + jnp.dot(piece, tall_in[...], preferred_element_type=F32)
+    inlet_part = jnp.sum(plan_in[...].astype(F32) * sums, axis=0, keepdims=True)
     read_part = finish_states()
     small_send[pl.ds(0, 1), :] = inlet_part
     small_send[pl.ds(1, 1), :] = read_part
@@ -591,26 +662,28 @@
     for d in range(1, tiles):
         small_copy(d).start()
 
+    dims = (((1,), (1,)), ((), ()))
+    inside = lax.dot_general(plan_out[...], tall_out[...], dims, preferred_element_type=F32)
+    final = warm[3, pl.ds(1, NX), pl.ds(8, NY), :].reshape(NX * NY, NZ)
+    heat_out[...] = (final - mixing * (inside * final)).reshape(NX, NY, NZ)
+
+    @pl.loop(1, NX - 1)
+    def _(x):
+        stream_plane(x)
+
     take_all(2)
 
-    @pl.loop(0, NX)
-    def _(x):
-        for i, (cx, cy, cz) in enumerate(VELOCITY):
-            v = grid[0, i, x + 1 - cx, pl.ds(8 - cy, NY), :]
-            f_out[i, x] = shifted_z(v, cz)
+    @pl.loop(0, 2)
+    def _(j):
+        stream_plane(j * (NX - 1))
+
+    for lanes, halo, row in ((Y_UP, LOW, 0), (Y_DOWN, TOP, NY - 1)):
+        for lane in lanes:
+            cx, _, cz = VELOCITY[lane]
+            v = grid[0, lane, pl.ds(1 - cx, NX), halo, :]
+            f_out[lane, :, row, :] = shifted_z(v, cz)
 
     wait_send_all(x_copies(2) + y_copies(2) + c_copies(2))
-
-    column = label_col[...]
-    cols = pl.ds(pl.multiple_of(tile * 128, 128), 128)
-    gain = jnp.zeros((RACKS, 128), F32)
-    for k in range(KINDS):
-        gain = jnp.where(column == k, gain_ref[k : k + 1, cols], gain)
-    response = jnp.sum(gain_ref[...] * read_ref[...], axis=1, keepdims=True)
-    kinds = lax.broadcasted_iota(jnp.int32, (KINDS, 128), 0)
-    labels = label_ref[pl.ds(slab, 1), :]
-    response_row = jnp.sum(jnp.where(kinds == labels, response, 0.0), axis=0, keepdims=True)
-    plan, tall = face_masks(outlet_ref[...], slab, tile, tiles)
 
     for d in range(1, tiles):
         small_copy(d).wait()
@@ -618,32 +691,40 @@
     for d in range(1, tiles):
         total = total + small_recv[d]
     inlet = total[0:1, :] * (1.0 / FACE)
-    exhaust = total[1:2, :] + response_row * inlet
-    states_out[...] = base_ref[...] + gain * jnp.transpose(jnp.broadcast_to(inlet, (128, RACKS)))
-    dims = (((1,), (1,)), ((), ()))
-    spread = lax.dot_general(
-        plan * exhaust, tall, dims, precision=lax.Precision.HIGHEST, preferred_element_type=F32
-    )
-    inside = lax.dot_general(
-        plan.astype(BF16), tall.astype(BF16), dims, preferred_element_type=F32
-    )
-    final = warm[3, pl.ds(1, NX), pl.ds(8, NY), :].reshape(NX * NY, NZ)
-    result = final + mixing * (spread - inside * final)
-    heat_out[...] = result.reshape(NX, NY, NZ)
+    exhaust = mixing * (total[1:2, :] + response[0:1, :] * inlet)
+    spread = jnp.zeros((NX * NY, NZ), F32)
+    for piece in three_parts(exhaust):
+        spread = spread + lax.dot_general(
+            plan_out[...], tall_out[...] * piece, dims, preferred_element_type=F32
+        )
+    heat_out[...] = heat_out[...] + spread.reshape(NX, NY, NZ)
+    inlets = jnp.transpose(jnp.broadcast_to(inlet, (128, RACKS)))
+    states_out[...] = base_ref[...] + gain_rows[...] * inlets
+
+
+def flush(f_ref, heat_ref, states_ref, f_out, heat_out, states_out, sems):
+    copies = [
+        pltpu.make_async_copy(heat_ref, heat_out, sems.at[19]),
+        pltpu.make_async_copy(states_ref, states_out, sems.at[20]),
+    ]
+    for i in range(19):
+        copies.append(pltpu.make_async_copy(f_ref.at[i], f_out.at[i], sems.at[i]))
+    for c in copies:
+        c.start()
+    for c in copies:
+        c.wait()
 
 
 def per_device(slabs, tiles, f, heat, solid, label, inlet, outlet, matrix, gain, read, state):
     vmem = pl.BlockSpec(memory_space=pltpu.VMEM)
-    hbm = pl.BlockSpec(memory_space=pl.ANY)
+    hbm = pl.BlockSpec(memory_space=pltpu.HBM)
     dma = pltpu.SemaphoreType.DMA
-    return pl.pallas_call(
+    results = ((19, NX, NY, NZ), (NX, NY, NZ), (RACKS, 128))
+    operands = (f, heat, solid, label.reshape(8, 128), inlet.T, outlet.T, matrix, gain, read, state)
+    outs = pl.pallas_call(
         functools.partial(kernel, slabs, tiles),
-        out_shape=(
-            jax.ShapeDtypeStruct((19, NX, NY, NZ), F32),
-            jax.ShapeDtypeStruct((NX, NY, NZ), F32),
-            jax.ShapeDtypeStruct((RACKS, 128), F32),
-        ),
-        in_specs=[hbm, hbm, hbm, vmem, hbm, hbm, vmem, vmem, vmem, vmem],
+        out_shape=tuple(pltpu.VMEM(shape, F32) for shape in results),
+        in_specs=[hbm] * 10,
         out_specs=(vmem, vmem, vmem),
         scratch_shapes=[
             pltpu.VMEM((19, NX, NY, NZ), F32),
@@ -651,8 +732,13 @@
             pltpu.VMEM((4, NX + 2, ROWS, NZ), F32),
             pltpu.VMEM((3, NX, NY, NZ), F32),
             pltpu.VMEM((NX, NY, NZ), jnp.int32),
-            pltpu.VMEM((RACKS, FACE), jnp.int32),
-            pltpu.VMEM((RACKS, FACE), jnp.int32),
+            pltpu.VMEM((FACE, RACKS), jnp.int32),
+            pltpu.VMEM((FACE, RACKS), jnp.int32),
+            pltpu.VMEM((slabs, 128), jnp.int32),
+            pltpu.VMEM((KINDS, 128, 256), BF16),
+            pltpu.VMEM((KINDS, tiles * 128), F32),
+            pltpu.VMEM((KINDS, tiles * 128), F32),
+            pltpu.VMEM((RACKS, tiles * 128), BF16),
             pltpu.VMEM((3, 2, 5, NY, NZ), BF16),
             pltpu.VMEM((3, 2, 5, NY, NZ), BF16),
             pltpu.VMEM((3, 2, 5, NX, NZ), BF16),
@@ -661,7 +747,14 @@
             pltpu.VMEM((3, 2, NX, NZ), F32),
             pltpu.VMEM((3, 2, NX, NZ), F32),
             pltpu.VMEM((slabs, RACKS, 256), BF16),
-            pltpu.VMEM((RACKS, 128), jnp.int32),
+            pltpu.VMEM((slabs * RACKS, 128), jnp.int32),
+            pltpu.VMEM((NX * NY, RACKS), BF16),
+            pltpu.VMEM((NZ, RACKS), BF16),
+            pltpu.VMEM((NX * NY, RACKS), BF16),
+            pltpu.VMEM((NZ, RACKS), BF16),
+            pltpu.VMEM((RACKS, 128), F32),
+            pltpu.VMEM((RACKS, 128), F32),
+            pltpu.VMEM((8, 128), F32),
             pltpu.VMEM((slabs, RACKS, 128), F32),
             pltpu.VMEM((slabs // 2 - 1, 2, RACKS, 128), F32),
             pltpu.VMEM((2, RACKS, 128), F32),
@@ -671,7 +764,7 @@
             pltpu.VMEM((tiles, 8, 128), F32),
             dma((NX,)),
             dma((NX,)),
-            dma((3,)),
+            dma((8,)),
             dma((3, 2)),
             dma((3, 2)),
             dma((3, 2)),
@@ -690,9 +783,17 @@
             dma((tiles,)),
         ],
         compiler_params=pltpu.CompilerParams(
-            collective_id=0, has_side_effects=True, vmem_limit_bytes=56 * 1024 * 1024
+            collective_id=0, has_side_effects=True, vmem_limit_bytes=40 * 1024 * 1024
         ),
-    )(f, heat, solid, label.reshape(8, 128), inlet, outlet, matrix, gain, read, state)
+    )(*(pltpu.with_memory_space_constraint(a, pltpu.HBM) for a in operands))
+    return pl.pallas_call(
+        flush,
+        out_shape=tuple(jax.ShapeDtypeStruct(shape, F32) for shape in results),
+        in_specs=[vmem] * 3,
+        out_specs=(hbm,) * 3,
+        scratch_shapes=[dma((21,))],
+        compiler_params=pltpu.CompilerParams(vmem_limit_bytes=1024 * 1024),
+    )(*outs)
 
 
 def solution(mesh):

time: 60.2 us -> 42.5 us (0.71)
  local copies, waits for them, and re-layouts: 10.6 us -> 0 us
  Pallas kernels: 48.8 us -> 41.8 us
    unnamed x9 -> x0, local copies, waits for them, and re-layouts: 10.6 us -> none
    pallas_call x1 -> x2, Pallas kernels: 48.8 us -> 41.8 us  [the longest x1 39.2 us: per_device(): pl.pallas_call(functools.partial(kernel, slabs, tiles), out_shape=tuple((...]
where the time goes in v2:
time: 42.5 us; the launch traced here: 42.4 us
  Pallas kernels  41.8 us (98%)
  between operations  0.64 us (2%)
    pallas_call x1, Pallas kernels, per_device(): pl.pallas_call(functools.partial(kernel, slabs, tiles), out_shape=tuple((...  39.2 us
    pallas_call x1, Pallas kernels, per_device(): pl.pallas_call(flush, out_shape=tuple((jax.ShapeDtypeStruct(shape, F32) f...  2.52 us

profile of v2, /device:TPU:1, one launch (start us, length us, event | category | flops | bytes accessed | tf_op | source)
XLA Modules:
  0.0 42.4 jit_solution(5670758704507281633)
XLA Ops:
  0.6 39.2 %shard_map.121 = (f32[19,16,32,128]{3,2,1,0:T(8,128)S(1)}, f32[16,32,128]{2,1,0:T(8,128)S(1)}, f32[128,128]{1,0:T(8,128)S(1)}) custom-call(f32[19,16,32,128]{3,2,1,0:T(8,128)} %f_hbm.1, f32[16,32,128]{2,1,0:T(8,128)} %heat_hbm.1, s32[16,32,128]{2,1,0:T(8,128)} %solid_hbm.1, s32[8,128]{1,0:T(8,128)} %bitcast.5, s32[32,1024]{1,0:T(8,128)} %bitcast.3, ...), custom_call_target="tpu_custom_call" | custom-call | tf_op jit(solution)/shard_map/pallas_call | solution.py:724
  39.9 2.5 %shard_map.122 = (f32[19,16,32,128]{3,2,1,0:T(8,128)}, f32[16,32,128]{2,1,0:T(8,128)}, f32[128,128]{1,0:T(8,128)}) custom-call(f32[19,16,32,128]{3,2,1,0:T(8,128)S(1)} %get-tuple-element.6.f_ref, f32[16,32,128]{2,1,0:T(8,128)S(1)} %get-tuple-element.7.heat_ref, f32[128,128]{1,0:T(8,128)S(1)} %get-tuple-element.8.states_ref), custom_call_target="tpu_custom_call" | custom-call | tf_op jit(solution)/shard_map/pallas_call | solution.py:789

commit v3 on v2

--- a/solution.py
+++ b/solution.py
@@ -52,22 +52,24 @@
 FACE = 32
 
 
-def collide(f, heat, solid):
+def gather_moments(f):
+    even = [f[p] + f[p + 1] for p in range(1, 19, 2)]
+    odd = [f[p] - f[p + 1] for p in range(1, 19, 2)]
+    density = (
+        f[0]
+        + ((even[0] + even[1]) + (even[2] + even[3]))
+        + ((even[4] + even[5]) + (even[6] + even[7]))
+        + even[8]
+    )
+    flow_x = (odd[0] + odd[3]) + (odd[4] + odd[5]) + odd[6]
+    flow_y = (odd[1] + odd[3]) + (odd[7] - odd[4]) + odd[8]
+    flow_z = (odd[2] + odd[5]) + (odd[7] - odd[6]) - odd[8]
+    return f[0], even, odd, density, flow_x, flow_y, flow_z
+
+
+def relax(still, even, odd, density, flow_x, flow_y, flow_z, heat, solid):
     omega = 1.0 / relax_time
     keep = 1.0 - omega
-    even, odd = {}, {}
-    for p in range(1, 19, 2):
-        even[p] = f[p] + f[p + 1]
-        odd[p] = f[p] - f[p + 1]
-    density = (
-        f[0]
-        + ((even[1] + even[3]) + (even[5] + even[7]))
-        + ((even[9] + even[11]) + (even[13] + even[15]))
-        + even[17]
-    )
-    flow_x = (odd[1] + odd[7]) + (odd[9] + odd[11]) + odd[13]
-    flow_y = (odd[3] + odd[7]) + (odd[15] - odd[9]) + odd[17]
-    flow_z = (odd[5] + odd[11]) + (odd[15] - odd[13]) - odd[17]
     inverse = jnp.where(solid, 0.0, 1.0 / density)
     share = jnp.where(solid, 0.0, density * (omega / 18.0))
     even_part = jnp.where(solid, 0.5, 0.5 * keep)
@@ -98,11 +100,11 @@
         17: (myz - qyz, hy - hz),
     }
     g = [None] * 19
-    g[0] = f[0] * jnp.where(solid, 1.0, keep) + level * 6.0
+    g[0] = still * jnp.where(solid, 1.0, keep) + level * 6.0
     for p in range(1, 19, 2):
         same, turn = terms[p]
-        both = even[p] * even_part + same
-        half = odd[p] * odd_part + turn
+        both = even[p // 2] * even_part + same
+        half = odd[p // 2] * odd_part + turn
         g[p] = both + half
         g[p + 1] = both - half
     return g, (ux, uy, uz)
@@ -158,9 +160,11 @@
     heat_out,
     states_out,
     fin,
-    grid,
+    grid_even,
+    grid_odd,
     warm,
     vel,
+    mid,
     solid_ref,
     inlet_ref,
     outlet_ref,
@@ -189,7 +193,8 @@
     part_x,
     pair,
     part_y,
-    base_ref,
+    cross_send,
+    cross_recv,
     small_send,
     small_recv,
     load_sem,
@@ -212,6 +217,15 @@
     ms_sem,
     mr_sem,
 ):
+    grids = (grid_even, grid_odd)
+    flats = [g.reshape(19, (NX + 2) * ROWS, NZ) for g in grids]
+    warm_flat = warm.reshape(4, (NX + 2) * ROWS, NZ)
+    fin_flat = fin.reshape(19, NX * NY, NZ)
+    solid_flat = solid_ref.reshape(NX * NY, NZ)
+
+    def along_x(row, first=1, count=NX):
+        return pl.ds(first * ROWS + row, count, stride=ROWS)
+
     slab = lax.axis_index("slab")
     tile = lax.axis_index("tile")
     s_up, s_down = lax.rem(slab + 1, slabs), lax.rem(slab + slabs - 1, slabs)
@@ -225,10 +239,9 @@
     def plane_copy(x):
         return pltpu.make_async_copy(f_hbm.at[:, x], fin.at[:, x], load_sem.at[x])
 
-    def heat_copy(x):
-        return pltpu.make_async_copy(
-            heat_hbm.at[x], warm.at[0, x + 1, pl.ds(8, NY), :], heat_sem.at[x]
-        )
+    heat_copy = pltpu.make_async_copy(
+        heat_hbm, warm.at[0, pl.ds(1, NX), pl.ds(8, NY), :], heat_sem.at[0]
+    )
 
     solid_copy = pltpu.make_async_copy(solid_hbm, solid_ref, misc_sem.at[0])
     first_rack = pl.multiple_of(slab * RACKS, RACKS)
@@ -240,12 +253,11 @@
     )
     solid_copy.start()
 
-    @pl.loop(0, NX)
-    def _(x):
-        heat_copy(x).start()
-
+    heat_copy.start()
     plane_copy(0).start()
     plane_copy(NX - 1).start()
+    state_copy_in = pltpu.make_async_copy(state_hbm, state_ref, misc_sem.at[7])
+    state_copy_in.start()
 
     @pl.loop(1, NX - 1)
     def _(x):
@@ -255,8 +267,6 @@
     matrix_copy = pltpu.make_async_copy(matrix_hbm, matrix_ref, misc_sem.at[4])
     gain_copy = pltpu.make_async_copy(gain_hbm, gain_ref, misc_sem.at[5])
     read_copy = pltpu.make_async_copy(read_hbm, read_ref, misc_sem.at[6])
-    state_copy_in = pltpu.make_async_copy(state_hbm, state_ref, misc_sem.at[7])
-    state_copy_in.start()
     table_copies = (label_copy, inlet_copy, outlet_copy, gain_copy, read_copy, matrix_copy)
     for c in table_copies:
         c.start()
@@ -274,6 +284,11 @@
         pl.semaphore_signal(
             barrier, inc=1, device_id=(lax.rem(slab + d, slabs), tile), device_id_type=MESH
         )
+
+    @pl.loop(1, tiles)
+    def _(d):
+        to = (slab + 1 - 2 * s_minor, lax.rem(tile + d, tiles))
+        pl.semaphore_signal(barrier, inc=1, device_id=to, device_id_type=MESH)
 
     for ds in (s_up, s_down):
         for dt in (t_up, t_down):
@@ -309,7 +324,7 @@
             to = (s_up if cx > 0 else s_down, t_up if cy > 0 else t_down)
             out.append(
                 remote(
-                    grid.at[n % 2, lane, x, pl.ds(y, 8), :],
+                    grids[n % 2].at[lane, x, pl.ds(y, 8), :],
                     c_recv.at[n, k],
                     cs_sem.at[n, k],
                     cr_sem.at[n, k],
@@ -351,25 +366,40 @@
         for c in copies:
             c.wait_send()
 
-    def collide_block(n, x, yt):
-        rows = pl.ds(8 + 8 * yt, 8)
-        here = pl.ds(8 * yt, 8)
-        if n == 0:
-            f = [fin[i, x, here, :] for i in range(19)]
-        else:
-            old = (n - 1) % 2
-            f = []
-            for i, (cx, cy, cz) in enumerate(VELOCITY):
-                v = grid[old, i, x + 1 - cx, pl.ds(8 + 8 * yt - cy, 8), :]
-                f.append(shifted_z(v, cz))
-        heat = warm[n, x + 1, rows, :]
-        solid = solid_ref[x, here, :] == 1
-        g, u = collide(f, heat, solid)
-        new = n % 2
-        for i in range(19):
-            grid[new, i, x + 1, rows, :] = g[i]
-        for d in range(3):
-            vel[d, x, here, :] = u[d]
+    def keep_moments(slot, f):
+        still, even, odd, density, *flow = gather_moments(f)
+        for i, v in enumerate((still, density, *flow, *even, *odd)):
+            mid[slot, i] = v
+
+    def relax_kept(slot, heat, solid):
+        even = [mid[slot, 5 + i] for i in range(9)]
+        odd = [mid[slot, 14 + i] for i in range(9)]
+        still, density, *flow = [mid[slot, i] for i in range(5)]
+        return relax(still, even, odd, density, *flow, heat, solid)
+
+    def moments(n, blocks):
+        for k, (x, yt) in enumerate(blocks):
+            here = pl.ds(8 * yt, 8)
+            if n == 0:
+                f = [fin[i, x, here, :] for i in range(19)]
+            else:
+                f = []
+                for i, (cx, cy, cz) in enumerate(VELOCITY):
+                    v = grids[(n - 1) % 2][i, x + 1 - cx, pl.ds(8 + 8 * yt - cy, 8), :]
+                    f.append(shifted_z(v, cz))
+            keep_moments(k, f)
+
+    def relaxation(n, blocks):
+        for k, (x, yt) in enumerate(blocks):
+            rows = pl.ds(8 + 8 * yt, 8)
+            here = pl.ds(8 * yt, 8)
+            heat = warm[n, x + 1, rows, :]
+            solid = solid_ref[x, here, :] == 1
+            g, u = relax_kept(k, heat, solid)
+            for i in range(19):
+                grids[n % 2][i, x + 1, rows, :] = g[i]
+            for d in range(3):
+                vel[d, x, here, :] = u[d]
 
     def heat_block(n, x, yt):
         rows = pl.ds(8 + 8 * yt, 8)
@@ -394,12 +424,12 @@
         warm[n + 1, x + 1, rows, :] = jnp.where(solid, centre, centre + diffusion * laplace - carried)
 
     def send_heat_rows(n):
-        ty_send[n, 0] = warm[n, pl.ds(1, NX), TOP - 1, :]
-        ty_send[n, 1] = warm[n, pl.ds(1, NX), LOW + 1, :]
+        ty_send[n, 0] = warm_flat[n, along_x(TOP - 1), :]
+        ty_send[n, 1] = warm_flat[n, along_x(LOW + 1), :]
 
     def take_heat_rows(n):
-        warm[n, pl.ds(1, NX), LOW, :] = ty_recv[n, 0]
-        warm[n, pl.ds(1, NX), TOP, :] = ty_recv[n, 1]
+        warm_flat[n, along_x(LOW), :] = ty_recv[n, 0]
+        warm_flat[n, along_x(TOP), :] = ty_recv[n, 1]
 
     def heat_pass(n):
         copies = t_copies(n)
@@ -419,57 +449,89 @@
     def pack_x(n):
         own = pl.ds(8, NY)
         for k, lane in enumerate(X_UP):
-            x_send[n, 0, k] = grid[n % 2, lane, NX, own, :].astype(BF16)
+            x_send[n, 0, k] = grids[n % 2][lane, NX, own, :].astype(BF16)
         for k, lane in enumerate(X_DOWN):
-            x_send[n, 1, k] = grid[n % 2, lane, 1, own, :].astype(BF16)
-
-    def pack_y(n):
-        for k, lane in enumerate(Y_UP):
-            y_send[n, 0, k] = grid[n % 2, lane, pl.ds(1, NX), TOP - 1, :].astype(BF16)
-        for k, lane in enumerate(Y_DOWN):
-            y_send[n, 1, k] = grid[n % 2, lane, pl.ds(1, NX), LOW + 1, :].astype(BF16)
+            x_send[n, 1, k] = grids[n % 2][lane, 1, own, :].astype(BF16)
+
+    def first_rows(n):
+        parts = [(y, half) for y in (NY - 1, 0) for half in range(2)]
+        for k, (y, half) in enumerate(parts):
+            if n == 0:
+                f = [fin_flat[i, pl.ds(8 * half * NY + y, 8, stride=NY), :] for i in range(19)]
+            else:
+                f = []
+                for i, (cx, cy, cz) in enumerate(VELOCITY):
+                    rows = along_x(8 + y - cy, 8 * half + 1 - cx, 8)
+                    f.append(shifted_z(flats[(n - 1) % 2][i, rows, :], cz))
+            keep_moments(4 + k, f)
+        for d, lanes in enumerate((Y_UP, Y_DOWN)):
+            found = []
+            for half in range(2):
+                y = parts[2 * d][0]
+                heat = warm_flat[n, along_x(8 + y, 8 * half + 1, 8), :]
+                solid = solid_flat[pl.ds(8 * half * NY + y, 8, stride=NY), :] == 1
+                found.append(relax_kept(4 + 2 * d + half, heat, solid)[0])
+            for k, lane in enumerate(lanes):
+                both = jnp.concatenate([found[0][lane], found[1][lane]], axis=0)
+                y_send[n, d, k] = both.astype(BF16)
 
     def take_all(n):
         wait_recv_all(x_copies(n))
         own = pl.ds(8, NY)
         for k, lane in enumerate(X_UP):
-            grid[n % 2, lane, 0, own, :] = x_recv[n, 0, k].astype(F32)
+            grids[n % 2][lane, 0, own, :] = x_recv[n, 0, k].astype(F32)
         for k, lane in enumerate(X_DOWN):
-            grid[n % 2, lane, NX + 1, own, :] = x_recv[n, 1, k].astype(F32)
+            grids[n % 2][lane, NX + 1, own, :] = x_recv[n, 1, k].astype(F32)
         wait_recv_all(y_copies(n))
         for k, lane in enumerate(Y_UP):
-            grid[n % 2, lane, pl.ds(1, NX), LOW, :] = y_recv[n, 0, k].astype(F32)
+            flats[n % 2][lane, along_x(LOW), :] = y_recv[n, 0, k].astype(F32)
         for k, lane in enumerate(Y_DOWN):
-            grid[n % 2, lane, pl.ds(1, NX), TOP, :] = y_recv[n, 1, k].astype(F32)
+            flats[n % 2][lane, along_x(TOP), :] = y_recv[n, 1, k].astype(F32)
         wait_recv_all(c_copies(n))
         for k, (lane, cx, cy) in enumerate(CORNERS):
             x = 0 if cx > 0 else NX + 1
             y = LOW if cy > 0 else TOP
             row = 7 if cy > 0 else 0
-            grid[n % 2, lane, x, pl.ds(y, 1), :] = c_recv[n, k, pl.ds(row, 1), :]
+            grids[n % 2][lane, x, pl.ds(y, 1), :] = c_recv[n, k, pl.ds(row, 1), :]
+
+    def border(x):
+        return [(x, yt) for yt in range(4)]
+
+    def rim(j):
+        return [(1 + 2 * j + k, yt) for k in range(2) for yt in (0, 3)]
+
+    def core_rows(j):
+        return [(1 + 2 * j + k, yt) for k in range(2) for yt in (1, 2)]
+
+    last = NX // 2 - 2
 
     def edges(n):
-        @pl.loop(0, 2)
+        if n == 0:
+            plane_copy(0).wait()
+            plane_copy(NX - 1).wait()
+        moments(n, border(0))
+        relaxation(n, border(0))
+        moments(n, border(NX - 1))
+        relaxation(n, border(NX - 1))
+
+    def rims(n):
+        moments(n, rim(0))
+
+        @pl.loop(0, last)
         def _(j):
-            x = j * (NX - 1)
-            if n == 0:
-                plane_copy(x).wait()
-            for yt in range(4):
-                collide_block(n, x, yt)
-
-    def rims(n):
-        @pl.loop(1, NX - 1)
-        def _(x):
-            if n == 0:
-                plane_copy(x).wait()
-            for yt in (0, 3):
-                collide_block(n, x, yt)
+            relaxation(n, rim(j))
+            moments(n, rim(j + 1))
+
+        relaxation(n, rim(last))
+        moments(n, core_rows(0))
 
     def middle(n):
-        @pl.loop(1, NX - 1)
-        def _(x):
-            for yt in (1, 2):
-                collide_block(n, x, yt)
+        @pl.loop(0, last)
+        def _(j):
+            relaxation(n, core_rows(j))
+            moments(n, core_rows(j + 1))
+
+        relaxation(n, core_rows(last))
 
     def send_x(n):
         pack_x(n)
@@ -477,7 +539,7 @@
         start_all(c_copies(n))
 
     def send_y(n):
-        pack_y(n)
+        first_rows(n)
         start_all(y_copies(n))
 
     half_cols = 128
@@ -535,11 +597,9 @@
 
     def multiply():
         partner_copy().wait()
-
-        rows = 256
-
-        @pl.loop(0, slabs * RACKS // rows)
-        def _(m):
+        rows = 2 * RACKS
+
+        def one_pair(m):
             block = kept[pl.ds(2 * m, 2)].reshape(rows, 256)
             column = label_col[pl.ds(pl.multiple_of(m * rows, rows), rows), :]
             total = jnp.zeros((rows, 128), F32)
@@ -552,14 +612,39 @@
                 total = jnp.where(column == 2 * k2 + 1, product[:, 128:], total)
             part[pl.ds(2 * m, 2)] = total.reshape(2, RACKS, 128)
 
-        for d in range(1, majors):
+        pl.loop(0, majors)(one_pair)
+
+    def start_majors():
+        for d in (2, 1, 3):
             major_copy(d).start()
+
+    def state_rows():
+        cols = pl.ds(pl.multiple_of(tile * 128, 128), 128)
+        return keep_share * state_ref[:, cols].astype(F32)
 
     def reduce_major():
         for d in range(1, majors):
             major_copy(d).wait()
         pair[...] = ((part[pl.ds(2 * s_major, 2)] + part_x[0]) + part_x[1]) + part_x[2]
         minor_copy().start()
+        own = read_rows[0] * (state_rows() + pair[s_minor])
+        other = read_rows[1] * pair[1 - s_minor]
+        small_send[pl.ds(1, 1), :] = jnp.sum(jnp.transpose(own), axis=0, keepdims=True)
+        row = jnp.sum(jnp.transpose(other), axis=0, keepdims=True)
+        cross_send[...] = jnp.broadcast_to(row, (8, 128))
+
+        @pl.loop(0, tiles)
+        def _(d):
+            cross_copy(d).start()
+
+    def cross_copy(d):
+        return remote(
+            cross_send,
+            cross_recv.at[tile],
+            ms_sem.at[1],
+            mr_sem.at[1],
+            (slab + 1 - 2 * s_minor, lax.rem(tile + d, tiles)),
+        )
 
     def tables():
         for c in table_copies:
@@ -573,69 +658,77 @@
             rows = pl.ds(pl.multiple_of(b * RACKS, RACKS), RACKS)
             label_col[rows, :] = jnp.transpose(jnp.broadcast_to(labels, (RACKS, 128)))
 
+        cols = pl.ds(pl.multiple_of(tile * 128, 128), 128)
         column = label_col[pl.ds(first_rack, RACKS), :]
-        cols = pl.ds(pl.multiple_of(tile * 128, 128), 128)
+        beside = pl.multiple_of((slab + 1 - 2 * s_minor) * RACKS, RACKS)
+        column_beside = label_col[pl.ds(beside, RACKS), :]
         gain = jnp.zeros((RACKS, 128), F32)
         read = jnp.zeros((RACKS, 128), F32)
+        read_beside = jnp.zeros((RACKS, 128), F32)
         for k in range(KINDS):
             gain = jnp.where(column == k, gain_ref[k : k + 1, cols], gain)
             read = jnp.where(column == k, read_ref[k : k + 1, cols], read)
+            read_beside = jnp.where(column_beside == k, read_ref[k : k + 1, cols], read_beside)
         gain_rows[...] = gain
-        read_rows[...] = read
+        read_rows[0] = read
+        read_rows[1] = read_beside
         per_kind = jnp.sum(gain_ref[...] * read_ref[...], axis=1, keepdims=True)
         kinds = lax.broadcasted_iota(jnp.int32, (KINDS, 128), 0)
         labels = label_ref[pl.ds(slab, 1), :]
         row = jnp.sum(jnp.where(kinds == labels, per_kind, 0.0), axis=0, keepdims=True)
         response[...] = jnp.broadcast_to(row, (8, 128))
 
-    def finish_states():
-        minor_copy().wait()
-        cols = pl.ds(pl.multiple_of(tile * 128, 128), 128)
-        base = keep_share * state_ref[:, cols].astype(F32) + (pair[s_minor] + part_y[...])
-        base_ref[...] = base
-        return jnp.sum(jnp.transpose(read_rows[...] * base), axis=0, keepdims=True)
-
     def small_copy(d):
         return remote(
             small_send,
             small_recv.at[d],
-            ms_sem.at[d],
-            mr_sem.at[d],
+            ms_sem.at[0],
+            mr_sem.at[0],
             (slab, lax.rem(tile + d, tiles)),
         )
+
+    def small_wait():
+        others = small_recv.at[pl.ds(1, tiles - 1)]
+        pltpu.make_async_copy(others, others, ms_sem.at[0]).wait()
+        pltpu.make_async_copy(others, others, mr_sem.at[0]).wait()
+        pltpu.make_async_copy(cross_recv, cross_recv, ms_sem.at[1]).wait()
+        pltpu.make_async_copy(cross_recv, cross_recv, mr_sem.at[1]).wait()
 
     def stream_plane(x):
         for i, (cx, cy, cz) in enumerate(VELOCITY):
-            v = grid[0, i, x + 1 - cx, pl.ds(8 - cy, NY), :]
+            v = grids[0][i, x + 1 - cx, pl.ds(8 - cy, NY), :]
             f_out[i, x] = shifted_z(v, cz)
 
     solid_copy.wait()
 
-    @pl.loop(0, NX)
-    def _(x):
-        heat_copy(x).wait()
-
+    heat_copy.wait()
     edges(0)
-    rims(0)
-    pl.semaphore_wait(barrier, (tiles - 1) + (slabs - 1) + 4)
+    pl.semaphore_wait(barrier, 2 * (tiles - 1) + (slabs - 1) + 4)
+    state_copy_in.wait()
+    start_states()
     send_heat_rows(0)
     start_all(t_copies(0))
     send_x(0)
+
+    @pl.loop(1, NX - 1)
+    def _(x):
+        plane_copy(x).wait()
+
     send_y(0)
-    state_copy_in.wait()
-    start_states()
+    rims(0)
     middle(0)
     tables()
+    share_states()
     heat_pass(0)
-    share_states()
     take_all(0)
     wait_send_all(x_copies(0) + y_copies(0) + c_copies(0))
 
     edges(1)
     send_x(1)
-    rims(1)
     send_y(1)
     multiply()
+    start_majors()
+    rims(1)
     middle(1)
     heat_pass(1)
     take_all(1)
@@ -643,8 +736,8 @@
 
     edges(2)
     send_x(2)
+    send_y(2)
     rims(2)
-    send_y(2)
     reduce_major()
     middle(2)
     heat_pass(2)
@@ -654,12 +747,10 @@
     for piece in three_parts(final):
         sums = sums + jnp.dot(piece, tall_in[...], preferred_element_type=F32)
     inlet_part = jnp.sum(plan_in[...].astype(F32) * sums, axis=0, keepdims=True)
-    read_part = finish_states()
     small_send[pl.ds(0, 1), :] = inlet_part
-    small_send[pl.ds(1, 1), :] = read_part
-    small_send[pl.ds(2, 6), :] = jnp.zeros((6, 128), F32)
-
-    for d in range(1, tiles):
+
+    @pl.loop(1, tiles)
+    def _(d):
         small_copy(d).start()
 
     dims = (((1,), (1,)), ((), ()))
@@ -677,21 +768,24 @@
     def _(j):
         stream_plane(j * (NX - 1))
 
+    out_flat = f_out.reshape(19, NX * NY, NZ)
     for lanes, halo, row in ((Y_UP, LOW, 0), (Y_DOWN, TOP, NY - 1)):
         for lane in lanes:
             cx, _, cz = VELOCITY[lane]
-            v = grid[0, lane, pl.ds(1 - cx, NX), halo, :]
-            f_out[lane, :, row, :] = shifted_z(v, cz)
+            v = flats[0][lane, along_x(halo, 1 - cx), :]
+            out_flat[lane, pl.ds(row, NX, stride=NY), :] = shifted_z(v, cz)
 
     wait_send_all(x_copies(2) + y_copies(2) + c_copies(2))
 
-    for d in range(1, tiles):
-        small_copy(d).wait()
+    small_wait()
     total = small_send[...]
     for d in range(1, tiles):
         total = total + small_recv[d]
     inlet = total[0:1, :] * (1.0 / FACE)
-    exhaust = mixing * (total[1:2, :] + response[0:1, :] * inlet)
+    readout = total[1:2, :]
+    for d in range(tiles):
+        readout = readout + cross_recv[d, 0:1, :]
+    exhaust = mixing * (readout + response[0:1, :] * inlet)
     spread = jnp.zeros((NX * NY, NZ), F32)
     for piece in three_parts(exhaust):
         spread = spread + lax.dot_general(
@@ -699,7 +793,8 @@
         )
     heat_out[...] = heat_out[...] + spread.reshape(NX, NY, NZ)
     inlets = jnp.transpose(jnp.broadcast_to(inlet, (128, RACKS)))
-    states_out[...] = base_ref[...] + gain_rows[...] * inlets
+    minor_copy().wait()
+    states_out[...] = (state_rows() + (pair[s_minor] + part_y[...])) + gain_rows[...] * inlets
 
 
 def flush(f_ref, heat_ref, states_ref, f_out, heat_out, states_out, sems):
@@ -728,9 +823,11 @@
         out_specs=(vmem, vmem, vmem),
         scratch_shapes=[
             pltpu.VMEM((19, NX, NY, NZ), F32),
-            pltpu.VMEM((2, 19, NX + 2, ROWS, NZ), F32),
+            pltpu.VMEM((19, NX + 2, ROWS, NZ), F32),
+            pltpu.VMEM((19, NX + 2, ROWS, NZ), F32),
             pltpu.VMEM((4, NX + 2, ROWS, NZ), F32),
             pltpu.VMEM((3, NX, NY, NZ), F32),
+            pltpu.VMEM((8, 23, 8, NZ), F32),
             pltpu.VMEM((NX, NY, NZ), jnp.int32),
             pltpu.VMEM((FACE, RACKS), jnp.int32),
             pltpu.VMEM((FACE, RACKS), jnp.int32),
@@ -753,17 +850,18 @@
             pltpu.VMEM((NX * NY, RACKS), BF16),
             pltpu.VMEM((NZ, RACKS), BF16),
             pltpu.VMEM((RACKS, 128), F32),
-            pltpu.VMEM((RACKS, 128), F32),
+            pltpu.VMEM((2, RACKS, 128), F32),
             pltpu.VMEM((8, 128), F32),
             pltpu.VMEM((slabs, RACKS, 128), F32),
             pltpu.VMEM((slabs // 2 - 1, 2, RACKS, 128), F32),
             pltpu.VMEM((2, RACKS, 128), F32),
             pltpu.VMEM((RACKS, 128), F32),
-            pltpu.VMEM((RACKS, 128), F32),
+            pltpu.VMEM((8, 128), F32),
+            pltpu.VMEM((tiles, 8, 128), F32),
             pltpu.VMEM((8, 128), F32),
             pltpu.VMEM((tiles, 8, 128), F32),
             dma((NX,)),
-            dma((NX,)),
+            dma((1,)),
             dma((8,)),
             dma((3, 2)),
             dma((3, 2)),
@@ -779,8 +877,8 @@
             dma((3,)),
             dma((1,)),
             dma((1,)),
-            dma((tiles,)),
-            dma((tiles,)),
+            dma((2,)),
+            dma((2,)),
         ],
         compiler_params=pltpu.CompilerParams(
             collective_id=0, has_side_effects=True, vmem_limit_bytes=40 * 1024 * 1024

time: 42.5 us -> 39.9 us (0.939)
  Pallas kernels: 41.8 us -> 39.1 us
    pallas_call x1, Pallas kernels: 39.2 us -> 36.6 us  [per_device(): pl.pallas_call(functools.partial(kernel, slabs, tiles), out_shape=tuple((...]
where the time goes in v3:
time: 39.9 us; the launch traced here: 39.8 us
  Pallas kernels  39.1 us (98%)
  between operations  0.64 us (2%)
    pallas_call x1, Pallas kernels, per_device(): pl.pallas_call(functools.partial(kernel, slabs, tiles), out_shape=tuple((...  36.6 us
    pallas_call x1, Pallas kernels, per_device(): pl.pallas_call(flush, out_shape=tuple((jax.ShapeDtypeStruct(shape, F32) f...  2.52 us

profile of v3, /device:TPU:1, one launch (start us, length us, event | category | flops | bytes accessed | tf_op | source)
XLA Modules:
  0.0 39.8 jit_solution(2415766760343794269)
XLA Ops:
  0.6 36.6 %shard_map.121 = (f32[19,16,32,128]{3,2,1,0:T(8,128)S(1)}, f32[16,32,128]{2,1,0:T(8,128)S(1)}, f32[128,128]{1,0:T(8,128)S(1)}) custom-call(f32[19,16,32,128]{3,2,1,0:T(8,128)} %f_hbm.1, f32[16,32,128]{2,1,0:T(8,128)} %heat_hbm.1, s32[16,32,128]{2,1,0:T(8,128)} %solid_hbm.1, s32[8,128]{1,0:T(8,128)} %bitcast.5, s32[32,1024]{1,0:T(8,128)} %bitcast.3, ...), custom_call_target="tpu_custom_call" | custom-call | tf_op jit(solution)/shard_map/pallas_call | solution.py:819
  37.3 2.5 %shard_map.122 = (f32[19,16,32,128]{3,2,1,0:T(8,128)}, f32[16,32,128]{2,1,0:T(8,128)}, f32[128,128]{1,0:T(8,128)}) custom-call(f32[19,16,32,128]{3,2,1,0:T(8,128)S(1)} %get-tuple-element.6.f_ref, f32[16,32,128]{2,1,0:T(8,128)S(1)} %get-tuple-element.7.heat_ref, f32[128,128]{1,0:T(8,128)S(1)} %get-tuple-element.8.states_ref), custom_call_target="tpu_custom_call" | custom-call | tf_op jit(solution)/shard_map/pallas_call | solution.py:887

commit v4 on v3

--- a/solution.py
+++ b/solution.py
@@ -165,6 +165,7 @@
     warm,
     vel,
     mid,
+    mid_all,
     solid_ref,
     inlet_ref,
     outlet_ref,
@@ -180,6 +181,7 @@
     c_recv,
     ty_send,
     ty_recv,
+    stage,
     kept,
     label_col,
     plan_in,
@@ -259,17 +261,11 @@
     state_copy_in = pltpu.make_async_copy(state_hbm, state_ref, misc_sem.at[7])
     state_copy_in.start()
 
-    @pl.loop(1, NX - 1)
-    def _(x):
-        plane_copy(x).start()
-
     label_copy = pltpu.make_async_copy(label_hbm, label_ref, misc_sem.at[3])
     matrix_copy = pltpu.make_async_copy(matrix_hbm, matrix_ref, misc_sem.at[4])
     gain_copy = pltpu.make_async_copy(gain_hbm, gain_ref, misc_sem.at[5])
     read_copy = pltpu.make_async_copy(read_hbm, read_ref, misc_sem.at[6])
     table_copies = (label_copy, inlet_copy, outlet_copy, gain_copy, read_copy, matrix_copy)
-    for c in table_copies:
-        c.start()
 
     barrier = pltpu.get_barrier_semaphore()
 
@@ -366,15 +362,16 @@
         for c in copies:
             c.wait_send()
 
-    def keep_moments(slot, f):
+    def keep_moments(slot, f, store=mid):
         still, even, odd, density, *flow = gather_moments(f)
         for i, v in enumerate((still, density, *flow, *even, *odd)):
-            mid[slot, i] = v
-
-    def relax_kept(slot, heat, solid):
-        even = [mid[slot, 5 + i] for i in range(9)]
-        odd = [mid[slot, 14 + i] for i in range(9)]
-        still, density, *flow = [mid[slot, i] for i in range(5)]
+            store[slot, i] = v
+        return density, flow
+
+    def relax_kept(slot, heat, solid, store=mid):
+        even = [store[slot, 5 + i] for i in range(9)]
+        odd = [store[slot, 14 + i] for i in range(9)]
+        still, density, *flow = [store[slot, i] for i in range(5)]
         return relax(still, even, odd, density, *flow, heat, solid)
 
     def moments(n, blocks):
@@ -509,6 +506,13 @@
         if n == 0:
             plane_copy(0).wait()
             plane_copy(NX - 1).wait()
+
+            @pl.loop(1, NX - 1)
+            def _(x):
+                plane_copy(x).start()
+
+            for c in table_copies:
+                c.start()
         moments(n, border(0))
         relaxation(n, border(0))
         moments(n, border(NX - 1))
@@ -533,6 +537,31 @@
 
         relaxation(n, core_rows(last))
 
+    def inner_moments(n):
+        @pl.loop(0, last + 1)
+        def _(j):
+            for k, (x, yt) in enumerate(rim(j) + core_rows(j)):
+                f = []
+                for i, (cx, cy, cz) in enumerate(VELOCITY):
+                    v = grids[(n - 1) % 2][i, x + 1 - cx, pl.ds(8 + 8 * yt - cy, 8), :]
+                    f.append(shifted_z(v, cz))
+                density, flow = keep_moments(8 * j + k, f, mid_all)
+                solid = solid_ref[x, pl.ds(8 * yt, 8), :] == 1
+                inverse = jnp.where(solid, 0.0, 1.0 / density)
+                for d in range(3):
+                    vel[d, x, pl.ds(8 * yt, 8), :] = flow[d] * inverse
+
+    def inner_relaxation(n):
+        @pl.loop(0, last + 1)
+        def _(j):
+            for k, (x, yt) in enumerate(rim(j) + core_rows(j)):
+                rows = pl.ds(8 + 8 * yt, 8)
+                heat = warm[n, x + 1, rows, :]
+                solid = solid_ref[x, pl.ds(8 * yt, 8), :] == 1
+                g, _ = relax_kept(8 * j + k, heat, solid, mid_all)
+                for i in range(19):
+                    grids[n % 2][i, x + 1, rows, :] = g[i]
+
     def send_x(n):
         pack_x(n)
         start_all(x_copies(n))
@@ -543,33 +572,25 @@
         start_all(y_copies(n))
 
     half_cols = 128
-    my_half = pl.ds(pl.multiple_of(core * half_cols, half_cols), half_cols)
 
     def state_copy(d):
         to = lax.rem(slab + d, slabs)
-        cols = pl.ds(pl.multiple_of(to * 256 + core * half_cols, half_cols), half_cols)
         return remote(
-            state_ref.at[:, cols],
-            kept.at[slab, :, my_half],
-            hs_sem.at[d],
-            hr_sem.at[d],
-            (to, tile),
+            stage.at[to], kept.at[core, slab], hs_sem.at[d], hr_sem.at[d], (to, tile)
         )
 
     def partner_copy():
         return remote(
-            kept.at[:, :, my_half],
-            kept.at[:, :, my_half],
-            hs_sem.at[0],
-            hr_sem.at[0],
-            (slab, partner),
+            kept.at[core], kept.at[core], hs_sem.at[0], hr_sem.at[0], (slab, partner)
         )
 
     def start_states():
+        for b in range(slabs):
+            cols = pl.ds(pl.multiple_of(b * 256 + core * half_cols, half_cols), half_cols)
+            stage[b] = state_ref[:, cols]
         for d in range(1, slabs):
             state_copy(d).start()
-        mine = pl.ds(pl.multiple_of(slab * 256 + core * half_cols, half_cols), half_cols)
-        kept[slab, :, my_half] = state_ref[:, mine]
+        kept[core, slab] = stage[slab]
 
     def share_states():
         for d in range(1, slabs):
@@ -600,7 +621,9 @@
         rows = 2 * RACKS
 
         def one_pair(m):
-            block = kept[pl.ds(2 * m, 2)].reshape(rows, 256)
+            block = jnp.concatenate(
+                [kept[c, pl.ds(2 * m, 2)].reshape(rows, 128) for c in range(2)], axis=1
+            )
             column = label_col[pl.ds(pl.multiple_of(m * rows, rows), rows), :]
             total = jnp.zeros((rows, 128), F32)
             for k2 in range(KINDS // 2):
@@ -612,11 +635,13 @@
                 total = jnp.where(column == 2 * k2 + 1, product[:, 128:], total)
             part[pl.ds(2 * m, 2)] = total.reshape(2, RACKS, 128)
 
-        pl.loop(0, majors)(one_pair)
-
-    def start_majors():
-        for d in (2, 1, 3):
+        @pl.loop(0, majors - 1)
+        def _(j):
+            d = jnp.where(j == 0, 2, jnp.where(j == 1, 1, 3))
+            one_pair(lax.rem(s_major + d, majors))
             major_copy(d).start()
+
+        one_pair(s_major)
 
     def state_rows():
         cols = pl.ds(pl.multiple_of(tile * 128, 128), 128)
@@ -727,7 +752,6 @@
     send_x(1)
     send_y(1)
     multiply()
-    start_majors()
     rims(1)
     middle(1)
     heat_pass(1)
@@ -737,21 +761,24 @@
     edges(2)
     send_x(2)
     send_y(2)
-    rims(2)
+    inner_moments(2)
     reduce_major()
-    middle(2)
     heat_pass(2)
 
     final = warm[3, pl.ds(1, NX), pl.ds(8, NY), :].reshape(NX * NY, NZ)
-    sums = jnp.zeros((NX * NY, RACKS), F32)
-    for piece in three_parts(final):
-        sums = sums + jnp.dot(piece, tall_in[...], preferred_element_type=F32)
+    sums = jnp.dot(
+        jnp.concatenate(three_parts(final), axis=1),
+        jnp.concatenate([tall_in[...]] * 3, axis=0),
+        preferred_element_type=F32,
+    )
     inlet_part = jnp.sum(plan_in[...].astype(F32) * sums, axis=0, keepdims=True)
     small_send[pl.ds(0, 1), :] = inlet_part
 
     @pl.loop(1, tiles)
     def _(d):
         small_copy(d).start()
+
+    inner_relaxation(2)
 
     dims = (((1,), (1,)), ((), ()))
     inside = lax.dot_general(plan_out[...], tall_out[...], dims, preferred_element_type=F32)
@@ -786,11 +813,12 @@
     for d in range(tiles):
         readout = readout + cross_recv[d, 0:1, :]
     exhaust = mixing * (readout + response[0:1, :] * inlet)
-    spread = jnp.zeros((NX * NY, NZ), F32)
-    for piece in three_parts(exhaust):
-        spread = spread + lax.dot_general(
-            plan_out[...], tall_out[...] * piece, dims, preferred_element_type=F32
-        )
+    spread = lax.dot_general(
+        jnp.concatenate([plan_out[...]] * 3, axis=1),
+        jnp.concatenate([tall_out[...] * piece for piece in three_parts(exhaust)], axis=1),
+        dims,
+        preferred_element_type=F32,
+    )
     heat_out[...] = heat_out[...] + spread.reshape(NX, NY, NZ)
     inlets = jnp.transpose(jnp.broadcast_to(inlet, (128, RACKS)))
     minor_copy().wait()
@@ -828,6 +856,7 @@
             pltpu.VMEM((4, NX + 2, ROWS, NZ), F32),
             pltpu.VMEM((3, NX, NY, NZ), F32),
             pltpu.VMEM((8, 23, 8, NZ), F32),
+            pltpu.VMEM((4 * (NX - 2), 23, 8, NZ), F32),
             pltpu.VMEM((NX, NY, NZ), jnp.int32),
             pltpu.VMEM((FACE, RACKS), jnp.int32),
             pltpu.VMEM((FACE, RACKS), jnp.int32),
@@ -843,7 +872,8 @@
             pltpu.VMEM((3, 4, 8, NZ), F32),
             pltpu.VMEM((3, 2, NX, NZ), F32),
             pltpu.VMEM((3, 2, NX, NZ), F32),
-            pltpu.VMEM((slabs, RACKS, 256), BF16),
+            pltpu.VMEM((slabs, RACKS, 128), BF16),
+            pltpu.VMEM((2, slabs, RACKS, 128), BF16),
             pltpu.VMEM((slabs * RACKS, 128), jnp.int32),
             pltpu.VMEM((NX * NY, RACKS), BF16),
             pltpu.VMEM((NZ, RACKS), BF16),
@@ -881,7 +911,7 @@
             dma((2,)),
         ],
         compiler_params=pltpu.CompilerParams(
-            collective_id=0, has_side_effects=True, vmem_limit_bytes=40 * 1024 * 1024
+            collective_id=0, has_side_effects=True, vmem_limit_bytes=46 * 1024 * 1024
         ),
     )(*(pltpu.with_memory_space_constraint(a, pltpu.HBM) for a in operands))
     return pl.pallas_call(

time: 39.9 us -> 39.8 us (level)
  no operation moved by 1% of the time
where the time goes in v4:
time: 39.8 us; the launch traced here: 39.7 us
  Pallas kernels  39 us (98%)
  between operations  0.64 us (2%)
    pallas_call x1, Pallas kernels, per_device(): pl.pallas_call(functools.partial(kernel, slabs, tiles), out_shape=tuple((...  36.5 us
    pallas_call x1, Pallas kernels, per_device(): pl.pallas_call(flush, out_shape=tuple((jax.ShapeDtypeStruct(shape, F32) f...  2.52 us

profile of v4, /device:TPU:1, one launch (start us, length us, event | category | flops | bytes accessed | tf_op | source)
XLA Modules:
  0.0 39.7 jit_solution(6733413821411647495)
XLA Ops:
  0.6 36.5 %shard_map.121 = (f32[19,16,32,128]{3,2,1,0:T(8,128)S(1)}, f32[16,32,128]{2,1,0:T(8,128)S(1)}, f32[128,128]{1,0:T(8,128)S(1)}) custom-call(f32[19,16,32,128]{3,2,1,0:T(8,128)} %f_hbm.1, f32[16,32,128]{2,1,0:T(8,128)} %heat_hbm.1, s32[16,32,128]{2,1,0:T(8,128)} %solid_hbm.1, s32[8,128]{1,0:T(8,128)} %bitcast.5, s32[32,1024]{1,0:T(8,128)} %bitcast.3, ...), custom_call_target="tpu_custom_call" | custom-call | tf_op jit(solution)/shard_map/pallas_call | solution.py:847
  37.1 2.5 %shard_map.122 = (f32[19,16,32,128]{3,2,1,0:T(8,128)}, f32[16,32,128]{2,1,0:T(8,128)}, f32[128,128]{1,0:T(8,128)}) custom-call(f32[19,16,32,128]{3,2,1,0:T(8,128)S(1)} %get-tuple-element.6.f_ref, f32[16,32,128]{2,1,0:T(8,128)S(1)} %get-tuple-element.7.heat_ref, f32[128,128]{1,0:T(8,128)S(1)} %get-tuple-element.8.states_ref), custom_call_target="tpu_custom_call" | custom-call | tf_op jit(solution)/shard_map/pallas_call | solution.py:917
